TPU v7x, 256 devices: a whole 4x4x8 slice. The times are simulated.
256 devices in a mesh: section: 8 (over x, core), blk: 32 (over y, z).
Axes of the slice: x: 4, y: 4, z: 8, core: 2. Of those that a mesh axis runs over, the one named last changes fastest.
Arguments:
- hidden: bfloat16 [16384, 1536], P('blk'), may hold values from -6 to 6
- stale_kv: bfloat16 [8, 16384, 3072], P('section', 'blk'), may hold values from -6 to 6
- w_qkv: bfloat16 [8, 1536, 4608], P('section', 'blk'), may hold values from -0.15625 to 0.15625
- w_out: bfloat16 [8, 1536, 1536], P('section', 'blk'), may hold values from -0.15625 to 0.15625
- q_gain: float32 [8, 128], P('section'), may hold values from 0.25 to 1.75
- k_gain: float32 [8, 128], P('section'), may hold values from 0.25 to 1.75
- mod_table: float32 [8, 16, 3, 1536], P('section'), may hold values from -4 to 4
- pattern: int32 [128, 8], P('blk'), may hold values from 0 to 1, as said below
- step_index: int32 [128], P('blk'), may hold values from 0 to 15
- order: int32 [4], replicated, may hold values from 0 to 3, each once
Outputs:
- layer_out: bfloat16 [8, 16384, 1536], P('section', 'blk')
- kv_cache: bfloat16 [8, 16384, 3072], P('section', 'blk')
Inputs may be any that keep to these rules, and one draw needn't show every extreme that they name: `pattern`: every row of the query tile's own tile (candidate c = tile index mod 4) is 1. `order`: names each patch once.
All inputs are finite; a program needn't handle non-finite values.
Results may differ from a plain program's by a relative error of at most 0.01.
Values may be sent and summed in bfloat16 or wider, within the bound.
A program may use at most 128 MiB of HBM per device.

v0:
```python
import math

import jax
import jax.numpy as jnp
from jax import lax
from jax.sharding import PartitionSpec as P

D = 1536
HEADS = 12
HDIM = 128
TILE = 128
PATCHES = 4
TSTEPS = 16
TOK_DEV = 128


NORM_EPS = 1e-06


def shifted(value, axis, steps):
    count = lax.axis_size(axis)
    pairs = [(source, (source + steps) % count) for source in range(count)]
    return lax.ppermute(value, axis, pairs)


def shifted_2(x, axis, by):
    count = lax.axis_size(axis)
    pairs = [(i, i + by) for i in range(count) if 0 <= i + by < count]
    return lax.ppermute(x, axis, pairs)


def layer_norm(values):
    centre = values - jnp.mean(values, axis=-1, keepdims=True)
    spread = jnp.mean(centre * centre, axis=-1, keepdims=True)
    return centre * lax.rsqrt(spread + NORM_EPS)


def head_norm(values, gain_row):
    square = jnp.mean(values * values, axis=-1, keepdims=True)
    return values * lax.rsqrt(square + NORM_EPS) * gain_row


def on_device(
    hidden, stale_kv, w_qkv, w_out, q_gain, k_gain, mod_table, pattern, step_index, order
):
    inner_width = HEADS * HDIM
    rows_patch = TOK_DEV
    tiles_patch = rows_patch // TILE
    candidate_tiles = pattern.shape[1]
    sections = lax.axis_size("section")
    section_id = lax.axis_index("section")
    full_qkv, full_out = (
        lax.all_gather(w_qkv[0], "blk", axis=0, tiled=True),
        lax.all_gather(w_out[0], "blk", axis=0, tiled=True),
    )
    query_gain = q_gain[0]
    key_gain = k_gain[0]
    modulation_table = mod_table[0].reshape(TSTEPS, 3 * D)
    tile_masks = pattern.reshape(PATCHES, tiles_patch, candidate_tiles)
    steps_tiles = step_index.reshape(PATCHES, tiles_patch)
    input_rows = hidden.reshape(PATCHES, rows_patch, D)
    own_store = stale_kv[0].reshape(PATCHES, rows_patch, 2 * inner_width)
    near_store = shifted(own_store, "blk", 1)
    received = jnp.zeros((rows_patch, D), jnp.bfloat16)
    results = jnp.zeros((PATCHES, rows_patch, D), jnp.bfloat16)
    inverse_root = 1.0 / math.sqrt(HDIM)

    def slot_step(slot, state_now):
        received, own_store, near_store, results = state_now
        offset = slot - section_id
        active = jnp.logical_and(offset >= 0, offset < PATCHES)
        clipped = jnp.clip(offset, 0, PATCHES - 1)
        patch_id = jnp.sum(jnp.where(jnp.arange(PATCHES) == clipped, order, 0))
        tokens = jnp.where(
            section_id == 0,
            lax.dynamic_index_in_dim(input_rows, patch_id, 0, keepdims=False),
            received,
        )
        tile_steps = lax.dynamic_index_in_dim(steps_tiles, patch_id, 0, keepdims=False)
        one_hot = (tile_steps[:, None] == jnp.arange(TSTEPS)[None, :]).astype(jnp.float32)
        modulation = jnp.dot(one_hot, modulation_table, precision=lax.Precision.HIGHEST)
        modulation = jnp.broadcast_to(modulation[:, None, :], (tiles_patch, TILE, 3 * D)).reshape(
            rows_patch, 3 * D
        )
        shift_term = modulation[:, :D]
        scale_term = modulation[:, D : 2 * D]
        gate_term = modulation[:, 2 * D :]

        def project(token_rows):
            modulated = (
                layer_norm(token_rows.astype(jnp.float32)) * (1.0 + scale_term) + shift_term
            ).astype(jnp.bfloat16)
            qkv = jnp.dot(modulated, full_qkv, preferred_element_type=jnp.float32)
            queries = head_norm(
                qkv[:, :inner_width].reshape(rows_patch, HEADS, HDIM), query_gain
            ).astype(jnp.bfloat16)
            return (modulated, queries, qkv[:, inner_width:].astype(jnp.bfloat16))

        def spare_project(token_rows):
            return (
                jnp.zeros((rows_patch, D), jnp.bfloat16),
                jnp.zeros((rows_patch, HEADS, HDIM), jnp.bfloat16),
                jnp.zeros((rows_patch, 2 * inner_width), jnp.bfloat16),
            )

        modulated, queries, fresh_kv = lax.cond(active, project, spare_project, tokens)
        own_store = jnp.where(
            active, lax.dynamic_update_index_in_dim(own_store, fresh_kv, patch_id, 0), own_store
        )
        near_fresh = shifted(fresh_kv, "blk", 1)
        near_store = jnp.where(
            active, lax.dynamic_update_index_in_dim(near_store, near_fresh, patch_id, 0), near_store
        )
        tile_mask = lax.dynamic_index_in_dim(tile_masks, patch_id, 0, keepdims=False)

        def attend(operands):
            token_rows, query_rows, own_rows, near_rows = operands
            candidates = jnp.concatenate(
                [own_rows.reshape(-1, 2 * inner_width), near_rows.reshape(-1, 2 * inner_width)],
                axis=0,
            )
            key_rows = head_norm(
                candidates[:, :inner_width].astype(jnp.float32).reshape(-1, HEADS, HDIM), key_gain
            ).astype(jnp.bfloat16)
            value_rows = candidates[:, inner_width:].reshape(-1, HEADS, HDIM)
            token_mask = jnp.broadcast_to(
                tile_mask.astype(jnp.float32)[:, None, :, None],
                (tiles_patch, TILE, candidate_tiles, TILE),
            ).reshape(rows_patch, candidate_tiles * TILE)
            scores = (
                jnp.einsum("qhd,khd->hqk", query_rows, key_rows, preferred_element_type=jnp.float32)
                * inverse_root
            )
            expo = jnp.exp(scores) * token_mask[None]
            weight_sum = jnp.sum(expo, axis=-1)
            mixture = jnp.einsum(
                "hqk,khd->qhd",
                expo.astype(jnp.bfloat16),
                value_rows,
                preferred_element_type=jnp.float32,
            )
            attended = (
                (mixture / jnp.transpose(weight_sum)[:, :, None])
                .reshape(rows_patch, inner_width)
                .astype(jnp.bfloat16)
            )
            projected = jnp.dot(attended, full_out, preferred_element_type=jnp.float32)
            return (token_rows.astype(jnp.float32) + gate_term * projected).astype(jnp.bfloat16)

        def spare_attend(operands):
            return jnp.zeros((rows_patch, D), jnp.bfloat16)

        output_rows = lax.cond(
            active, attend, spare_attend, (tokens, queries, own_store, near_store)
        )
        results = jnp.where(
            active, lax.dynamic_update_index_in_dim(results, output_rows, patch_id, 0), results
        )
        received = shifted_2(output_rows, "section", 1)
        return (received, own_store, near_store, results)

    slot_count = PATCHES + sections - 1
    received, own_store, near_store, results = lax.fori_loop(
        0, slot_count, slot_step, (received, own_store, near_store, results)
    )
    layer_out = results.reshape(1, PATCHES * rows_patch, D)
    kv_cache = own_store.reshape(1, PATCHES * rows_patch, 2 * inner_width)
    return (layer_out, kv_cache)


def solution(mesh):
    in_specs = (
        P("blk", None),
        P("section", "blk", None),
        P("section", "blk", None),
        P("section", "blk", None),
        P("section", None),
        P("section", None),
        P("section", None, None, None),
        P("blk", None),
        P("blk"),
        P(),
    )
    out_specs = (P("section", "blk", None), P("section", "blk", None))
    return jax.shard_map(
        on_device, mesh=mesh, in_specs=in_specs, out_specs=out_specs, check_vma=False
    )
```

profile of v0, /device:TPU:103, one launch (start us, length us, event | category | flops | bytes accessed | tf_op | source)
XLA Modules:
  0.0 1014.6 jit_solution(15740919164373035649)
XLA Ops:
  7.2 3.8 copy.63
  15.8 93.7 %collective-permute-done.2 = bf16[4,128,3072]{2,1,0:T(8,128)(2,1)} collective-permute-done((bf16[4,128,3072]{2,1,0:T(8,128)(2,1)}, bf16[4,128,3072]{2,1,0:T(8,128)(2,1)}, u32[]{:S(2)}, u32[]{:S(2)}) %collective-permute-start.2) | collective-permute-done | bytes 3145760 | tf_op jit(solution)/shard_map/ppermute | solution.py:23
  110.1 129.9 %all-gather.5.cloned.1.call-done = bf16[1,1536,4608]{2,1,0:T(8,128)(2,1)} async-done(((bf16[1,48,4608]{2,1,0:T(8,128)(2,1)}), bf16[1,1536,4608]{2,1,0:T(8,128)(2,1)}) %all-gather.5.cloned.1.call-update) | async-done | bytes 14155792 | tf_op jit(solution)/shard_map/all_gather | solution.py:53
  241.3 766.4 %while.20 = (s32[]{:T(128)}, bf16[128,1536]{1,0:T(8,128)(2,1)S(1)}, bf16[4,128,3072]{2,1,0:T(8,128)(2,1)}, bf16[4,128,3072]{2,1,0:T(8,128)(2,1)}, bf16[4,128,153...) while((s32[]{:T(128)}, bf16[128,1536]{1,0:T(8,128)(2,1)S(1)}, ...), condition=%wide.region_11.12_spmd, body=%wide.region_0.11_spmd.sunk | while | flops 3260855808 | bytes 107183792 | solution.py:163
  253.3 15.6 %collective-permute-done = bf16[128,3072]{1,0:T(8,128)(2,1)S(1)} collective-permute-done((bf16[128,3072]{1,0:T(8,128)(2,1)}, bf16[128,3072]{1,0:T(8,128)(2,1)S(1)}, u32[]{:S(2)}, u32[]{:S(2)}) %collective-permute-start) | collective-permute-done | bytes 786464 | tf_op jit(solution)/shard_map/while/body/eval_jaxpr/ppermute | solution.py:23
  291.2 9.5 collective-permute-done
  307.5 7.1 collective-permute-done.1
  329.0 7.9 collective-permute-done
  343.8 8.2 collective-permute-done.1
  366.9 9.0 collective-permute-done
  382.7 7.1 collective-permute-done.1
  404.8 9.5 collective-permute-done
  421.1 6.8 collective-permute-done.1
  442.6 11.6 %collective-permute-done = bf16[128,3072]{1,0:T(8,128)(2,1)S(1)} collective-permute-done((bf16[128,3072]{1,0:T(8,128)(2,1)}, bf16[128,3072]{1,0:T(8,128)(2,1)S(1)}, u32[]{:S(2)}, u32[]{:S(2)}) %collective-permute-start) | collective-permute-done | bytes 786464 | tf_op jit(solution)/shard_map/while/body/eval_jaxpr/ppermute | solution.py:23
  461.1 6.8 collective-permute-done.1
  480.5 11.2 %collective-permute-done = bf16[128,3072]{1,0:T(8,128)(2,1)S(1)} collective-permute-done((bf16[128,3072]{1,0:T(8,128)(2,1)}, bf16[128,3072]{1,0:T(8,128)(2,1)S(1)}, u32[]{:S(2)}, u32[]{:S(2)}) %collective-permute-start) | collective-permute-done | bytes 786464 | tf_op jit(solution)/shard_map/while/body/eval_jaxpr/ppermute | solution.py:23
  498.6 209.0 %collective-permute-done.1 = bf16[128,1536]{1,0:T(8,128)(2,1)S(1)} collective-permute-done((bf16[128,1536]{1,0:T(8,128)(2,1)}, bf16[128,1536]{1,0:T(8,128)(2,1)S(1)}, u32[]{:S(2)}, u32[]{:S(2)}) %collective-permute-start.1) | collective-permute-done | bytes 393248 | tf_op jit(solution)/shard_map/while/body/eval_jaxpr/ppermute | solution.py:29
  714.1 13.7 %conditional.4 = (bf16[128,12,128]{0,2,1:T(8,128)(2,1)}, bf16[128,3072]{1,0:T(8,128)(2,1)}, bf16[1,128,3072]{2,1,0:T(8,128)(2,1)}) conditional(s32[]{:T(128)} %convert_element_type.92, () %tuple.70, (bf16[128,1536]{1,0:T(8,128)(2,1)S(1)}, f32[4608]{0:T(1024)}, bf16[1536,4608]{1,0:T(8,128)(2,1)}, f32[1,128]{1,0:T(1,128)S(1)}) %tuple.71), branch_computations={%region_2.2_spmd, %region_3.6_spmd} | conditional | flops 1815284864 | bytes 26018840 | solution.py:106
  715.3 7.2 fusion.6
  730.3 12.2 %collective-permute-done = bf16[128,3072]{1,0:T(8,128)(2,1)S(1)} collective-permute-done((bf16[128,3072]{1,0:T(8,128)(2,1)}, bf16[128,3072]{1,0:T(8,128)(2,1)S(1)}, u32[]{:S(2)}, u32[]{:S(2)}) %collective-permute-start) | collective-permute-done | bytes 786464 | tf_op jit(solution)/shard_map/while/body/eval_jaxpr/ppermute | solution.py:23
  744.7 24.4 %conditional.5 = (bf16[128,1536]{1,0:T(8,128)(2,1)}, bf16[1,128,1536]{2,1,0:T(8,128)(2,1)}) conditional(s32[]{:T(128)} %convert_element_type.92, () %tuple.69, (bf16[128,1536]{1,0:T(8,128)(2,1)S(1)}, f32[4608]{0:T(1024)}, bf16[4,128,3072]{2,1,0:T(8,128)(2,1)}, bf16[4,128,3072]{2,1,0:T(8,128)(2,1)}, f32[1,128]{1,0:T(1,128)S(1)}, ...), branch_computations={%region_7.7_spmd, %region_8.10_spmd} | conditional | flops 1443506688 | bytes 69053088 | solution.py:153
  747.9 4.7 copy.31
  752.6 5.6 pad_maximum_fusion
  759.8 3.3 bitcast_reduce_fusion
  772.4 10.1 collective-permute-done.1
  789.1 13.7 %conditional.4 = (bf16[128,12,128]{0,2,1:T(8,128)(2,1)}, bf16[128,3072]{1,0:T(8,128)(2,1)}, bf16[1,128,3072]{2,1,0:T(8,128)(2,1)}) conditional(s32[]{:T(128)} %convert_element_type.92, () %tuple.70, (bf16[128,1536]{1,0:T(8,128)(2,1)S(1)}, f32[4608]{0:T(1024)}, bf16[1536,4608]{1,0:T(8,128)(2,1)}, f32[1,128]{1,0:T(1,128)S(1)}) %tuple.71), branch_computations={%region_2.2_spmd, %region_3.6_spmd} | conditional | flops 1815284864 | bytes 26018840 | solution.py:106
  790.3 7.1 fusion.6
  805.3 12.2 %collective-permute-done = bf16[128,3072]{1,0:T(8,128)(2,1)S(1)} collective-permute-done((bf16[128,3072]{1,0:T(8,128)(2,1)}, bf16[128,3072]{1,0:T(8,128)(2,1)S(1)}, u32[]{:S(2)}, u32[]{:S(2)}) %collective-permute-start) | collective-permute-done | bytes 786464 | tf_op jit(solution)/shard_map/while/body/eval_jaxpr/ppermute | solution.py:23
  819.7 24.4 %conditional.5 = (bf16[128,1536]{1,0:T(8,128)(2,1)}, bf16[1,128,1536]{2,1,0:T(8,128)(2,1)}) conditional(s32[]{:T(128)} %convert_element_type.92, () %tuple.69, (bf16[128,1536]{1,0:T(8,128)(2,1)S(1)}, f32[4608]{0:T(1024)}, bf16[4,128,3072]{2,1,0:T(8,128)(2,1)}, bf16[4,128,3072]{2,1,0:T(8,128)(2,1)}, f32[1,128]{1,0:T(1,128)S(1)}, ...), branch_computations={%region_7.7_spmd, %region_8.10_spmd} | conditional | flops 1443506688 | bytes 69053088 | solution.py:153
  822.9 4.7 copy.31
  827.6 5.6 pad_maximum_fusion
  834.8 3.3 bitcast_reduce_fusion
  847.4 12.0 %collective-permute-done.1 = bf16[128,1536]{1,0:T(8,128)(2,1)S(1)} collective-permute-done((bf16[128,1536]{1,0:T(8,128)(2,1)}, bf16[128,1536]{1,0:T(8,128)(2,1)S(1)}, u32[]{:S(2)}, u32[]{:S(2)}) %collective-permute-start.1) | collective-permute-done | bytes 393248 | tf_op jit(solution)/shard_map/while/body/eval_jaxpr/ppermute | solution.py:29
  866.0 13.7 %conditional.4 = (bf16[128,12,128]{0,2,1:T(8,128)(2,1)}, bf16[128,3072]{1,0:T(8,128)(2,1)}, bf16[1,128,3072]{2,1,0:T(8,128)(2,1)}) conditional(s32[]{:T(128)} %convert_element_type.92, () %tuple.70, (bf16[128,1536]{1,0:T(8,128)(2,1)S(1)}, f32[4608]{0:T(1024)}, bf16[1536,4608]{1,0:T(8,128)(2,1)}, f32[1,128]{1,0:T(1,128)S(1)}) %tuple.71), branch_computations={%region_2.2_spmd, %region_3.6_spmd} | conditional | flops 1815284864 | bytes 26018840 | solution.py:106
  867.2 7.1 fusion.6
  882.1 12.2 %collective-permute-done = bf16[128,3072]{1,0:T(8,128)(2,1)S(1)} collective-permute-done((bf16[128,3072]{1,0:T(8,128)(2,1)}, bf16[128,3072]{1,0:T(8,128)(2,1)S(1)}, u32[]{:S(2)}, u32[]{:S(2)}) %collective-permute-start) | collective-permute-done | bytes 786464 | tf_op jit(solution)/shard_map/while/body/eval_jaxpr/ppermute | solution.py:23
  896.6 24.4 %conditional.5 = (bf16[128,1536]{1,0:T(8,128)(2,1)}, bf16[1,128,1536]{2,1,0:T(8,128)(2,1)}) conditional(s32[]{:T(128)} %convert_element_type.92, () %tuple.69, (bf16[128,1536]{1,0:T(8,128)(2,1)S(1)}, f32[4608]{0:T(1024)}, bf16[4,128,3072]{2,1,0:T(8,128)(2,1)}, bf16[4,128,3072]{2,1,0:T(8,128)(2,1)}, f32[1,128]{1,0:T(1,128)S(1)}, ...), branch_computations={%region_7.7_spmd, %region_8.10_spmd} | conditional | flops 1443506688 | bytes 69053088 | solution.py:153
  899.8 4.7 copy.31
  904.5 5.6 pad_maximum_fusion
  911.7 3.3 bitcast_reduce_fusion
  924.2 14.4 %collective-permute-done.1 = bf16[128,1536]{1,0:T(8,128)(2,1)S(1)} collective-permute-done((bf16[128,1536]{1,0:T(8,128)(2,1)}, bf16[128,1536]{1,0:T(8,128)(2,1)S(1)}, u32[]{:S(2)}, u32[]{:S(2)}) %collective-permute-start.1) | collective-permute-done | bytes 393248 | tf_op jit(solution)/shard_map/while/body/eval_jaxpr/ppermute | solution.py:29
  945.2 13.7 %conditional.4 = (bf16[128,12,128]{0,2,1:T(8,128)(2,1)}, bf16[128,3072]{1,0:T(8,128)(2,1)}, bf16[1,128,3072]{2,1,0:T(8,128)(2,1)}) conditional(s32[]{:T(128)} %convert_element_type.92, () %tuple.70, (bf16[128,1536]{1,0:T(8,128)(2,1)S(1)}, f32[4608]{0:T(1024)}, bf16[1536,4608]{1,0:T(8,128)(2,1)}, f32[1,128]{1,0:T(1,128)S(1)}) %tuple.71), branch_computations={%region_2.2_spmd, %region_3.6_spmd} | conditional | flops 1815284864 | bytes 26018840 | solution.py:106
  946.4 7.1 fusion.6
  961.4 15.9 %collective-permute-done = bf16[128,3072]{1,0:T(8,128)(2,1)S(1)} collective-permute-done((bf16[128,3072]{1,0:T(8,128)(2,1)}, bf16[128,3072]{1,0:T(8,128)(2,1)S(1)}, u32[]{:S(2)}, u32[]{:S(2)}) %collective-permute-start) | collective-permute-done | bytes 786464 | tf_op jit(solution)/shard_map/while/body/eval_jaxpr/ppermute | solution.py:23
  979.5 24.4 %conditional.5 = (bf16[128,1536]{1,0:T(8,128)(2,1)}, bf16[1,128,1536]{2,1,0:T(8,128)(2,1)}) conditional(s32[]{:T(128)} %convert_element_type.92, () %tuple.69, (bf16[128,1536]{1,0:T(8,128)(2,1)S(1)}, f32[4608]{0:T(1024)}, bf16[4,128,3072]{2,1,0:T(8,128)(2,1)}, bf16[4,128,3072]{2,1,0:T(8,128)(2,1)}, f32[1,128]{1,0:T(1,128)S(1)}, ...), branch_computations={%region_7.7_spmd, %region_8.10_spmd} | conditional | flops 1443506688 | bytes 69053088 | solution.py:153
  982.7 4.7 copy.31
  987.4 5.6 pad_maximum_fusion
  994.6 3.3 bitcast_reduce_fusion
  (274 shorter events, 291.4 us)
Async XLA Ops:
  7.2 7.6 copy-start
  7.2 102.9 %all-gather.7.cloned.1.call-start = ((), (), s32[]{:S(2)}) async-start(), calls=%async_computation.1 | async-start | bytes 4866048 | tf_op jit(solution)/shard_map/all_gather | solution.py:54
  11.0 230.2 %copy-start.1 = (f32[1,128]{1,0:T(1,128)S(1)}, f32[1,128]{1,0:T(1,128)}, u32[]{:S(2)}) copy-start(f32[1,128]{1,0:T(1,128)} %param.20) | copy-start | bytes 1540
  11.0 230.2 %copy-start.2 = (s32[4]{0:T(128)S(1)}, s32[4]{0:T(128)}, u32[]{:S(2)}) copy-start(s32[4]{0:T(128)} %param.25) | copy-start | bytes 52
  11.0 230.2 %copy-start.3 = (s32[4]{0:T(128)S(1)}, s32[4]{0:T(128)}, u32[]{:S(2)}) copy-start(s32[4]{0:T(128)} %param.24) | copy-start | bytes 52
  11.0 230.2 %copy-start.4 = (f32[1,128]{1,0:T(1,128)S(1)}, f32[1,128]{1,0:T(1,128)}, u32[]{:S(2)}) copy-start(f32[1,128]{1,0:T(1,128)} %param.21) | copy-start | bytes 1540
  11.0 228.9 %all-gather.5.cloned.1.call-start = ((), (), s32[]{:S(2)}) async-start(), calls=%async_computation | async-start | bytes 14598144 | tf_op jit(solution)/shard_map/all_gather | solution.py:53
  11.8 97.7 %collective-permute-start.2 = (bf16[4,128,3072]{2,1,0:T(8,128)(2,1)}, bf16[4,128,3072]{2,1,0:T(8,128)(2,1)}, u32[]{:S(2)}, u32[]{:S(2)}) collective-permute-start(bf16[4,128,3072]{2,1,0:T(8,128)(2,1)} %bitcast.20), channel_id=1, source_target_pairs={{0,1},{1,2},{2,3},{3,4},{4,5},{5,6},{6,7},{7,8},{8,9},{9,10},{10,1... | collective-permute-start | bytes 9437192 | tf_op jit(solution)/shard_map/ppermute | solution.py:23
  250.7 18.2 %collective-permute-start = (bf16[128,3072]{1,0:T(8,128)(2,1)}, bf16[128,3072]{1,0:T(8,128)(2,1)S(1)}, u32[]{:S(2)}, u32[]{:S(2)}) collective-permute-start(bf16[128,3072]{1,0:T(8,128)(2,1)} %get-tuple-element.585), channel_id=1, source_target_pairs={{0,1},{1,2},{2,3},{3,4},{4,5},{5,6},{6,7},{7,8},{8,9},{9,10},{10,1... | collective-permute-start | bytes 2359304 | tf_op jit(solution)/shard_map/while/body/eval_jaxpr/ppermute | solution.py:23
  272.7 5.3 collective-permute-start.1
  287.4 13.3 %collective-permute-start = (bf16[128,3072]{1,0:T(8,128)(2,1)}, bf16[128,3072]{1,0:T(8,128)(2,1)S(1)}, u32[]{:S(2)}, u32[]{:S(2)}) collective-permute-start(bf16[128,3072]{1,0:T(8,128)(2,1)} %get-tuple-element.585), channel_id=1, source_target_pairs={{0,1},{1,2},{2,3},{3,4},{4,5},{5,6},{6,7},{7,8},{8,9},{9,10},{10,1... | collective-permute-start | bytes 2359304 | tf_op jit(solution)/shard_map/while/body/eval_jaxpr/ppermute | solution.py:23
  304.4 10.2 %collective-permute-start.1 = (bf16[128,1536]{1,0:T(8,128)(2,1)}, bf16[128,1536]{1,0:T(8,128)(2,1)S(1)}, u32[]{:S(2)}, u32[]{:S(2)}) collective-permute-start(bf16[128,1536]{1,0:T(8,128)(2,1)} %get-tuple-element.587), channel_id=1, source_target_pairs={{0,32},{32,64},{64,96},{96,128},{128,160},{160,192},{192,224},{1,3... | collective-permute-start | bytes 1179656 | tf_op jit(solution)/shard_map/while/body/eval_jaxpr/ppermute | solution.py:29
  324.0 12.9 %collective-permute-start = (bf16[128,3072]{1,0:T(8,128)(2,1)}, bf16[128,3072]{1,0:T(8,128)(2,1)S(1)}, u32[]{:S(2)}, u32[]{:S(2)}) collective-permute-start(bf16[128,3072]{1,0:T(8,128)(2,1)} %get-tuple-element.585), channel_id=1, source_target_pairs={{0,1},{1,2},{2,3},{3,4},{4,5},{5,6},{6,7},{7,8},{8,9},{9,10},{10,1... | collective-permute-start | bytes 2359304 | tf_op jit(solution)/shard_map/while/body/eval_jaxpr/ppermute | solution.py:23
  340.6 11.3 %collective-permute-start.1 = (bf16[128,1536]{1,0:T(8,128)(2,1)}, bf16[128,1536]{1,0:T(8,128)(2,1)S(1)}, u32[]{:S(2)}, u32[]{:S(2)}) collective-permute-start(bf16[128,1536]{1,0:T(8,128)(2,1)} %get-tuple-element.587), channel_id=1, source_target_pairs={{0,32},{32,64},{64,96},{96,128},{128,160},{160,192},{192,224},{1,3... | collective-permute-start | bytes 1179656 | tf_op jit(solution)/shard_map/while/body/eval_jaxpr/ppermute | solution.py:29
  361.4 14.5 %collective-permute-start = (bf16[128,3072]{1,0:T(8,128)(2,1)}, bf16[128,3072]{1,0:T(8,128)(2,1)S(1)}, u32[]{:S(2)}, u32[]{:S(2)}) collective-permute-start(bf16[128,3072]{1,0:T(8,128)(2,1)} %get-tuple-element.585), channel_id=1, source_target_pairs={{0,1},{1,2},{2,3},{3,4},{4,5},{5,6},{6,7},{7,8},{8,9},{9,10},{10,1... | collective-permute-start | bytes 2359304 | tf_op jit(solution)/shard_map/while/body/eval_jaxpr/ppermute | solution.py:23
  379.6 10.2 %collective-permute-start.1 = (bf16[128,1536]{1,0:T(8,128)(2,1)}, bf16[128,1536]{1,0:T(8,128)(2,1)S(1)}, u32[]{:S(2)}, u32[]{:S(2)}) collective-permute-start(bf16[128,1536]{1,0:T(8,128)(2,1)} %get-tuple-element.587), channel_id=1, source_target_pairs={{0,32},{32,64},{64,96},{96,128},{128,160},{160,192},{192,224},{1,3... | collective-permute-start | bytes 1179656 | tf_op jit(solution)/shard_map/while/body/eval_jaxpr/ppermute | solution.py:29
  399.2 15.0 %collective-permute-start = (bf16[128,3072]{1,0:T(8,128)(2,1)}, bf16[128,3072]{1,0:T(8,128)(2,1)S(1)}, u32[]{:S(2)}, u32[]{:S(2)}) collective-permute-start(bf16[128,3072]{1,0:T(8,128)(2,1)} %get-tuple-element.585), channel_id=1, source_target_pairs={{0,1},{1,2},{2,3},{3,4},{4,5},{5,6},{6,7},{7,8},{8,9},{9,10},{10,1... | collective-permute-start | bytes 2359304 | tf_op jit(solution)/shard_map/while/body/eval_jaxpr/ppermute | solution.py:23
  418.0 9.9 collective-permute-start.1
  437.4 16.9 %collective-permute-start = (bf16[128,3072]{1,0:T(8,128)(2,1)}, bf16[128,3072]{1,0:T(8,128)(2,1)S(1)}, u32[]{:S(2)}, u32[]{:S(2)}) collective-permute-start(bf16[128,3072]{1,0:T(8,128)(2,1)} %get-tuple-element.585), channel_id=1, source_target_pairs={{0,1},{1,2},{2,3},{3,4},{4,5},{5,6},{6,7},{7,8},{8,9},{9,10},{10,1... | collective-permute-start | bytes 2359304 | tf_op jit(solution)/shard_map/while/body/eval_jaxpr/ppermute | solution.py:23
  458.0 9.9 collective-permute-start.1
  477.3 14.4 %collective-permute-start = (bf16[128,3072]{1,0:T(8,128)(2,1)}, bf16[128,3072]{1,0:T(8,128)(2,1)S(1)}, u32[]{:S(2)}, u32[]{:S(2)}) collective-permute-start(bf16[128,3072]{1,0:T(8,128)(2,1)} %get-tuple-element.585), channel_id=1, source_target_pairs={{0,1},{1,2},{2,3},{3,4},{4,5},{5,6},{6,7},{7,8},{8,9},{9,10},{10,1... | collective-permute-start | bytes 2359304 | tf_op jit(solution)/shard_map/while/body/eval_jaxpr/ppermute | solution.py:23
  495.5 212.1 %collective-permute-start.1 = (bf16[128,1536]{1,0:T(8,128)(2,1)}, bf16[128,1536]{1,0:T(8,128)(2,1)S(1)}, u32[]{:S(2)}, u32[]{:S(2)}) collective-permute-start(bf16[128,1536]{1,0:T(8,128)(2,1)} %get-tuple-element.587), channel_id=1, source_target_pairs={{0,32},{32,64},{64,96},{96,128},{128,160},{160,192},{192,224},{1,3... | collective-permute-start | bytes 1179656 | tf_op jit(solution)/shard_map/while/body/eval_jaxpr/ppermute | solution.py:29
  727.9 14.6 %collective-permute-start = (bf16[128,3072]{1,0:T(8,128)(2,1)}, bf16[128,3072]{1,0:T(8,128)(2,1)S(1)}, u32[]{:S(2)}, u32[]{:S(2)}) collective-permute-start(bf16[128,3072]{1,0:T(8,128)(2,1)} %get-tuple-element.585), channel_id=1, source_target_pairs={{0,1},{1,2},{2,3},{3,4},{4,5},{5,6},{6,7},{7,8},{8,9},{9,10},{10,1... | collective-permute-start | bytes 2359304 | tf_op jit(solution)/shard_map/while/body/eval_jaxpr/ppermute | solution.py:23
  759.8 6.0 slice-start
  763.1 2.7 slice-start.1
  769.1 13.4 %collective-permute-start.1 = (bf16[128,1536]{1,0:T(8,128)(2,1)}, bf16[128,1536]{1,0:T(8,128)(2,1)S(1)}, u32[]{:S(2)}, u32[]{:S(2)}) collective-permute-start(bf16[128,1536]{1,0:T(8,128)(2,1)} %get-tuple-element.587), channel_id=1, source_target_pairs={{0,32},{32,64},{64,96},{96,128},{128,160},{160,192},{192,224},{1,3... | collective-permute-start | bytes 1179656 | tf_op jit(solution)/shard_map/while/body/eval_jaxpr/ppermute | solution.py:29
  802.8 14.6 %collective-permute-start = (bf16[128,3072]{1,0:T(8,128)(2,1)}, bf16[128,3072]{1,0:T(8,128)(2,1)S(1)}, u32[]{:S(2)}, u32[]{:S(2)}) collective-permute-start(bf16[128,3072]{1,0:T(8,128)(2,1)} %get-tuple-element.585), channel_id=1, source_target_pairs={{0,1},{1,2},{2,3},{3,4},{4,5},{5,6},{6,7},{7,8},{8,9},{9,10},{10,1... | collective-permute-start | bytes 2359304 | tf_op jit(solution)/shard_map/while/body/eval_jaxpr/ppermute | solution.py:23
  834.8 6.0 slice-start
  838.1 2.7 slice-start.1
  844.1 15.3 %collective-permute-start.1 = (bf16[128,1536]{1,0:T(8,128)(2,1)}, bf16[128,1536]{1,0:T(8,128)(2,1)S(1)}, u32[]{:S(2)}, u32[]{:S(2)}) collective-permute-start(bf16[128,1536]{1,0:T(8,128)(2,1)} %get-tuple-element.587), channel_id=1, source_target_pairs={{0,32},{32,64},{64,96},{96,128},{128,160},{160,192},{192,224},{1,3... | collective-permute-start | bytes 1179656 | tf_op jit(solution)/shard_map/while/body/eval_jaxpr/ppermute | solution.py:29
  879.7 14.7 %collective-permute-start = (bf16[128,3072]{1,0:T(8,128)(2,1)}, bf16[128,3072]{1,0:T(8,128)(2,1)S(1)}, u32[]{:S(2)}, u32[]{:S(2)}) collective-permute-start(bf16[128,3072]{1,0:T(8,128)(2,1)} %get-tuple-element.585), channel_id=1, source_target_pairs={{0,1},{1,2},{2,3},{3,4},{4,5},{5,6},{6,7},{7,8},{8,9},{9,10},{10,1... | collective-permute-start | bytes 2359304 | tf_op jit(solution)/shard_map/while/body/eval_jaxpr/ppermute | solution.py:23
  911.6 6.0 slice-start
  915.0 2.7 slice-start.1
  921.0 17.6 %collective-permute-start.1 = (bf16[128,1536]{1,0:T(8,128)(2,1)}, bf16[128,1536]{1,0:T(8,128)(2,1)S(1)}, u32[]{:S(2)}, u32[]{:S(2)}) collective-permute-start(bf16[128,1536]{1,0:T(8,128)(2,1)} %get-tuple-element.587), channel_id=1, source_target_pairs={{0,32},{32,64},{64,96},{96,128},{128,160},{160,192},{192,224},{1,3... | collective-permute-start | bytes 1179656 | tf_op jit(solution)/shard_map/while/body/eval_jaxpr/ppermute | solution.py:29
  958.9 18.3 %collective-permute-start = (bf16[128,3072]{1,0:T(8,128)(2,1)}, bf16[128,3072]{1,0:T(8,128)(2,1)S(1)}, u32[]{:S(2)}, u32[]{:S(2)}) collective-permute-start(bf16[128,3072]{1,0:T(8,128)(2,1)} %get-tuple-element.585), channel_id=1, source_target_pairs={{0,1},{1,2},{2,3},{3,4},{4,5},{5,6},{6,7},{7,8},{8,9},{9,10},{10,1... | collective-permute-start | bytes 2359304 | tf_op jit(solution)/shard_map/while/body/eval_jaxpr/ppermute | solution.py:23
  994.6 6.0 slice-start
  997.9 2.7 slice-start.1
  1003.9 3.8 collective-permute-start.1
Sparse Core Ops, SparseCore 0:
  11.2 98.8 all-gather.6
  112.6 127.2 all-gather.4
where the time goes:
time: 1030 us; the launch traced here: 1010 us
  waiting for transfers between devices  636 us (62%)
  other arithmetic  126 us (12%)
  local copies, waits for them, and re-layouts  103 us (10%)
  matrix products  82.5 us (8%)
  starting transfers between devices  32.5 us (3%)
  loops' own time  20.9 us (2%)
  between operations  14.1 us (1%)
    ppermute x11, waiting for transfers between devices, shifted_2(): return lax.ppermute(x, axis, pairs)  284 us
    ppermute x12, waiting for transfers between devices, shifted(): return lax.ppermute(value, axis, pairs)  221 us
    all_gather x1, waiting for transfers between devices, on_device(): lax.all_gather(w_qkv[0], 'blk', axis=0, tiled=True)  130 us
    dot_general x4, matrix products, project(): qkv = jnp.dot(modulated, full_qkv, preferred_element_type=jnp.float32)  28.6 us
    dot_general x11, matrix products, slot_step(): jnp.dot(one_hot, modulation_table, precision=lax.Precision.HIGHEST)  26.6 us
    select_n x11, other arithmetic, slot_step(): jnp.where(active, lax.dynamic_update_index_in_dim(own_store, fresh_kv, pa...  25.1 us
    select_n x11, other arithmetic, slot_step(): jnp.where(active, lax.dynamic_update_index_in_dim(near_store, near_fresh,...  24.1 us
    concatenate x4, other arithmetic, attend(): jnp.concatenate([own_rows.reshape(-1, 2 * inner_width), near_rows.reshape...  22.5 us
  transfers between devices with their start and end apart: 25, of which 25 were waited for; matrix products, arithmetic and copies ran while one was open for 5% of the time, Pallas kernels for 0%

commit v1 on v0

v1 whole, which is shorter than its diff:
```python
import math

import jax
import jax.numpy as jnp
from jax import lax
from jax.experimental import pallas as pl
from jax.experimental.pallas import tpu as pltpu
from jax.sharding import PartitionSpec as P

MESH = pl.DeviceIdType.MESH

D = 1536
HEADS = 12
HDIM = 128
PATCHES = 4
TSTEPS = 16
ROWS = 128
SEQ_DEV = PATCHES * ROWS
INNER = HEADS * HDIM
NY, NZ = 4, 8
NBLK = NY * NZ
NSEC = 8
SHARD = D // NBLK
NORM_EPS = 1e-06
CHUNK = 512
N_SEND = 70
SCORE_SCALE = math.log2(math.e) / math.sqrt(HDIM)


def head_norm(values, gain_row):
    square = jnp.mean(values * values, axis=-1, keepdims=True)
    return values * lax.rsqrt(square + NORM_EPS) * gain_row


def modulate(rows, scale, shift):
    values = rows.astype(jnp.float32)
    centre = values - jnp.mean(values, axis=-1, keepdims=True)
    spread = jnp.mean(centre * centre, axis=-1, keepdims=True)
    return (centre * lax.rsqrt(spread + NORM_EPS) * (1.0 + scale) + shift).astype(jnp.bfloat16)


def kernel(
    order_s, step_s, pattern_s, hidden_h, stale_h, wq_h, wo_h, qgain, kgain, mod_table,
    out_h, kv_h,
    wq, wo, keys, values, x_own, x_near, mod_own, mod_near, stale, hidden, fresh, out_rows, modulated, queries, attended,
    recv_q, recv_o, send, local, rx_own, rx_near, tx_own, tx_near, store_sem, rx_stale, tx_stale, rx_mod, tx_mod,
):
    sec = lax.axis_index("section")
    blk = lax.axis_index("blk")
    y, z = blk // NZ, lax.rem(blk, NZ)

    def at(yy, zz):
        return lax.rem(yy + 2 * NY, NY) * NZ + lax.rem(zz + 2 * NZ, NZ)

    up, down = lax.rem(sec + 1, NSEC), lax.rem(sec + NSEC - 1, NSEC)
    after, before = lax.rem(blk + 1, NBLK), lax.rem(blk + NBLK - 1, NBLK)
    zp, zm, yp, ym = at(y, z + 1), at(y, z - 1), at(y + 1, z), at(y - 1, z)

    load_hidden = pltpu.make_async_copy(hidden_h, hidden, local.at[0])
    load_stale = pltpu.make_async_copy(stale_h, stale, local.at[1])
    load_wq = pltpu.make_async_copy(wq_h, wq.at[pl.ds(blk * SHARD, SHARD)], local.at[2])
    load_wo = pltpu.make_async_copy(wo_h, wo.at[pl.ds(blk * SHARD, SHARD)], local.at[3])
    load_stale.start()
    load_hidden.start()
    load_wq.start()
    load_wo.start()

    barrier = pltpu.get_barrier_semaphore()
    for target in (
        (sec, zp), (sec, zm), (sec, yp), (sec, ym), (sec, after), (sec, before),
        (up, blk), (down, blk), (up, after), (down, before),
    ):
        pl.semaphore_signal(barrier, inc=1, device_id=target, device_id_type=MESH)
    pl.semaphore_wait(barrier, 10)

    sends = []

    def push(which, shard, target, source=None):
        buffer, recv = (wq, recv_q) if which == "q" else (wo, recv_o)
        rows = buffer.at[pl.ds(shard * SHARD, SHARD)]
        copy = pltpu.make_async_remote_copy(
            src_ref=rows if source is None else source,
            dst_ref=rows,
            send_sem=send.at[len(sends)],
            recv_sem=recv.at[shard],
            device_id=(sec, target),
            device_id_type=MESH,
        )
        copy.start()
        sends.append(copy)

    def arrived(which, shard):
        buffer, recv = (wq, recv_q) if which == "q" else (wo, recv_o)
        rows = buffer.at[pl.ds(shard * SHARD, SHARD)]
        pltpu.make_async_remote_copy(
            src_ref=rows, dst_ref=rows, send_sem=send.at[0], recv_sem=recv.at[shard],
            device_id=(sec, blk), device_id_type=MESH,
        ).wait_recv()

    push("o", blk, yp, wo_h)
    push("o", blk, ym, wo_h)
    push("q", blk, zp, wq_h)
    push("q", blk, zm, wq_h)
    push("q", blk, yp, wq_h)
    push("q", blk, ym, wq_h)
    push("o", blk, zp, wo_h)
    push("o", blk, zm, wo_h)

    for slot in range(PATCHES):
        step = step_s[order_s[slot]]
        for row in range(3):
            mod_own[slot, pl.ds(row, 1), :] = mod_table[pl.ds(3 * step + row, 1), :]
    send_mod = pltpu.make_async_remote_copy(
        src_ref=mod_own, dst_ref=mod_near, send_sem=tx_mod, recv_sem=rx_mod,
        device_id=(sec, after), device_id_type=MESH,
    )
    send_mod.start()

    load_hidden.wait()

    def near_copy(slot):
        return pltpu.make_async_remote_copy(
            src_ref=x_own.at[slot], dst_ref=x_near.at[slot], send_sem=tx_near.at[slot], recv_sem=rx_near.at[slot],
            device_id=(sec, after), device_id_type=MESH,
        )

    @pl.when(sec == 0)
    def _():
        for slot in range(PATCHES):
            x_own[slot] = hidden[order_s[slot]]
        for slot in range(PATCHES):
            near_copy(slot).start()

    load_stale.wait()
    for slot in range(1, PATCHES):
        patch = order_s[slot]
        for head in range(HEADS):
            columns = pl.ds(head * HDIM, HDIM)
            keys[pl.ds(slot * ROWS, ROWS), columns] = head_norm(
                stale[patch, :, columns].astype(jnp.float32), kgain[...]
            ).astype(jnp.bfloat16)
        values[pl.ds(slot * ROWS, ROWS), :] = stale[patch, :, INNER:]
    stale_sends = []
    for index, buffer in enumerate((keys, values)):
        copy = pltpu.make_async_remote_copy(
            src_ref=buffer.at[pl.ds(ROWS, SEQ_DEV - ROWS)],
            dst_ref=buffer.at[pl.ds(SEQ_DEV + ROWS, SEQ_DEV - ROWS)],
            send_sem=tx_stale.at[index], recv_sem=rx_stale.at[index],
            device_id=(sec, after), device_id_type=MESH,
        )
        copy.start()
        stale_sends.append(copy)

    even = lax.rem(z, 2) == 0
    arrived("o", ym)
    arrived("o", yp)
    push("o", jnp.where(even, ym, yp), jnp.where(even, yp, ym))
    for shard in (ym, yp):
        push("o", shard, zp)
        push("o", shard, zm)
    arrived("o", at(y + 2, z))
    push("o", at(y + 2, z), zp)
    push("o", at(y + 2, z), zm)

    def cross(zk):
        arrived("q", at(y - 1, zk))
        arrived("q", at(y + 1, zk))
        odd = lax.rem(zk + NZ, 2) == 1
        push("q", jnp.where(odd, at(y + 1, zk), at(y - 1, zk)), jnp.where(odd, ym, yp))

    previous = z
    for k in range(1, NZ):
        if k == NZ - 1:
            zk, forward = z + NZ // 2, None
        elif k % 2 == 1:
            zk, forward = z - (k + 1) // 2, (zp if k < NZ - 3 else None)
        else:
            zk, forward = z + k // 2, zm
        arrived("q", at(y, zk))
        if forward is not None:
            push("q", at(y, zk), forward)
        push("q", at(y, zk), yp)
        push("q", at(y, zk), ym)
        cross(previous)
        for i in range(NY):
            arrived("o", at(y + i, zk))
            if forward is not None:
                push("o", at(y + i, zk), forward)
        previous = zk
    cross(previous)
    for i in range(NZ):
        arrived("q", at(y + 2, z + i))
    load_wq.wait()
    load_wo.wait()
    send_mod.wait()
    for copy in stale_sends:
        copy.wait()

    def slot_step(slot, carry):
        @pl.when(sec > 0)
        def _():
            pltpu.make_async_remote_copy(
                src_ref=x_own.at[slot], dst_ref=x_own.at[slot], send_sem=tx_own.at[slot], recv_sem=rx_own.at[slot],
                device_id=(up, blk), device_id_type=MESH,
            ).wait_recv()

        modulated[pl.ds(0, ROWS), :] = modulate(
            x_own[slot], mod_own[slot, pl.ds(1, 1), :], mod_own[slot, pl.ds(0, 1), :]
        )
        near_copy(slot).wait_recv()
        modulated[pl.ds(ROWS, ROWS), :] = modulate(
            x_near[slot], mod_near[slot, pl.ds(1, 1), :], mod_near[slot, pl.ds(0, 1), :]
        )
        own_rows = pl.ds(pl.multiple_of(slot * ROWS, ROWS), ROWS)
        near_rows = pl.ds(pl.multiple_of(SEQ_DEV + slot * ROWS, ROWS), ROWS)

        def project_q(chunk, carry):
            base = pl.multiple_of(chunk * CHUNK, CHUNK)
            product = jnp.dot(
                modulated[pl.ds(0, ROWS), :], wq[:, pl.ds(base, CHUNK)], preferred_element_type=jnp.float32
            )
            for head in range(CHUNK // HDIM):
                queries[:, pl.ds(base + head * HDIM, HDIM)] = head_norm(
                    product[:, head * HDIM:(head + 1) * HDIM], qgain[...]
                ).astype(jnp.bfloat16)
            return carry

        def project_k(chunk, carry):
            base = pl.multiple_of(chunk * CHUNK, CHUNK)
            product = jnp.dot(
                modulated[...], wq[:, pl.ds(INNER + base, CHUNK)], preferred_element_type=jnp.float32
            ).astype(jnp.bfloat16)
            fresh[slot, :, pl.ds(base, CHUNK)] = product[:ROWS]
            for head in range(CHUNK // HDIM):
                normed = head_norm(
                    product[:, head * HDIM:(head + 1) * HDIM].astype(jnp.float32), kgain[...]
                ).astype(jnp.bfloat16)
                columns = pl.ds(base + head * HDIM, HDIM)
                keys[own_rows, columns] = normed[:ROWS]
                keys[near_rows, columns] = normed[ROWS:]
            return carry

        def project_v(chunk, carry):
            base = pl.multiple_of(chunk * CHUNK, CHUNK)
            product = jnp.dot(
                modulated[...], wq[:, pl.ds(2 * INNER + base, CHUNK)], preferred_element_type=jnp.float32
            ).astype(jnp.bfloat16)
            fresh[slot, :, pl.ds(INNER + base, CHUNK)] = product[:ROWS]
            values[own_rows, pl.ds(base, CHUNK)] = product[:ROWS]
            values[near_rows, pl.ds(base, CHUNK)] = product[ROWS:]
            return carry

        lax.fori_loop(0, INNER // CHUNK, project_q, 0)
        lax.fori_loop(0, INNER // CHUNK, project_k, 0)
        lax.fori_loop(0, INNER // CHUNK, project_v, 0)
        pltpu.make_async_copy(fresh.at[slot], kv_h.at[slot], store_sem.at[0, slot]).start()

        patch = order_s[slot]
        masks = [
            pattern_s[patch, half * PATCHES + order_s[j]].astype(jnp.float32) for half in range(2) for j in range(PATCHES)
        ]

        def attend(head, carry):
            columns = pl.ds(pl.multiple_of(head * HDIM, HDIM), HDIM)
            scores = lax.dot_general(
                queries[:, columns], keys[:, columns], (((1,), (1,)), ((), ())), preferred_element_type=jnp.float32
            )
            tiles = [
                jnp.exp2(scores[:, j * ROWS:(j + 1) * ROWS] * SCORE_SCALE) * masks[j] for j in range(2 * PATCHES)
            ]
            total = tiles[0]
            for tile in tiles[1:]:
                total = total + tile
            weight_sum = jnp.sum(total, axis=-1, keepdims=True)
            probs = jnp.concatenate([tile.astype(jnp.bfloat16) for tile in tiles], axis=1)
            mixture = jnp.dot(probs, values[:, columns], preferred_element_type=jnp.float32)
            attended[:, columns] = (mixture / weight_sum).astype(jnp.bfloat16)
            return carry

        lax.fori_loop(0, HEADS, attend, 0, unroll=2)

        def project_out(chunk, carry):
            columns = pl.ds(pl.multiple_of(chunk * CHUNK, CHUNK), CHUNK)
            product = jnp.dot(attended[...], wo[:, columns], preferred_element_type=jnp.float32)
            out_rows[slot, :, columns] = (
                x_own[slot, :, columns].astype(jnp.float32) + mod_own[slot, pl.ds(2, 1), columns] * product
            ).astype(jnp.bfloat16)
            return carry

        lax.fori_loop(0, D // CHUNK, project_out, 0)

        @pl.when(sec < NSEC - 1)
        def _():
            for target, landing, tx, rx in ((blk, x_own, tx_own, rx_own), (after, x_near, tx_near, rx_near)):
                pltpu.make_async_remote_copy(
                    src_ref=out_rows.at[slot], dst_ref=landing.at[slot], send_sem=tx.at[slot], recv_sem=rx.at[slot],
                    device_id=(up, target), device_id_type=MESH,
                ).start()

        pltpu.make_async_copy(out_rows.at[slot], out_h.at[slot], store_sem.at[1, slot]).start()
        return carry

    @pl.when(sec == 0)
    def _():
        for slot in range(PATCHES):
            near_copy(slot).wait_send()

    lax.fori_loop(0, PATCHES, slot_step, 0)

    for copy in sends:
        copy.wait_send()
    for slot in range(PATCHES):
        pltpu.make_async_copy(fresh.at[slot], kv_h.at[slot], store_sem.at[0, slot]).wait()
        pltpu.make_async_copy(out_rows.at[slot], out_h.at[slot], store_sem.at[1, slot]).wait()

    @pl.when(sec < NSEC - 1)
    def _():
        for slot in range(PATCHES):
            for tx in (tx_own, tx_near):
                pltpu.make_async_remote_copy(
                    src_ref=out_rows.at[slot], dst_ref=x_own.at[slot], send_sem=tx.at[slot], recv_sem=rx_own.at[slot],
                    device_id=(up, blk), device_id_type=MESH,
                ).wait_send()


def to_patch_order(order_s, rows_in, kv_in, rows_out, kv_out):
    rows_out[...] = rows_in[...]
    kv_out[...] = kv_in[...]


def on_device(hidden, stale_kv, w_qkv, w_out, q_gain, k_gain, mod_table, pattern, step_index, order):
    vmem, smem, anywhere = (
        pl.BlockSpec(memory_space=pltpu.VMEM),
        pl.BlockSpec(memory_space=pltpu.SMEM),
        pl.BlockSpec(memory_space=pl.ANY),
    )
    bf16, f32 = jnp.bfloat16, jnp.float32
    dma = pltpu.SemaphoreType.DMA
    rows_slots, kv_slots = pl.pallas_call(
        kernel,
        out_shape=(
            jax.ShapeDtypeStruct((PATCHES, ROWS, D), bf16),
            jax.ShapeDtypeStruct((PATCHES, ROWS, 2 * INNER), bf16),
        ),
        in_specs=[smem] * 3 + [anywhere] * 4 + [vmem] * 3,
        out_specs=(anywhere, anywhere),
        scratch_shapes=[
            pltpu.VMEM((D, 3 * INNER), bf16),
            pltpu.VMEM((INNER, D), bf16),
            pltpu.VMEM((2 * SEQ_DEV, INNER), bf16),
            pltpu.VMEM((2 * SEQ_DEV, INNER), bf16),
            pltpu.VMEM((PATCHES, ROWS, D), bf16),
            pltpu.VMEM((PATCHES, ROWS, D), bf16),
            pltpu.VMEM((PATCHES, 8, D), f32),
            pltpu.VMEM((PATCHES, 8, D), f32),
            pltpu.VMEM((PATCHES, ROWS, 2 * INNER), bf16),
            pltpu.VMEM((PATCHES, ROWS, D), bf16),
            pltpu.VMEM((PATCHES, ROWS, 2 * INNER), bf16),
            pltpu.VMEM((PATCHES, ROWS, D), bf16),
            pltpu.VMEM((2 * ROWS, D), bf16),
            pltpu.VMEM((ROWS, INNER), bf16),
            pltpu.VMEM((ROWS, INNER), bf16),
            dma((NBLK,)),
            dma((NBLK,)),
            dma((N_SEND,)),
            dma((4,)),
            dma((PATCHES,)),
            dma((PATCHES,)),
            dma((PATCHES,)),
            dma((PATCHES,)),
            dma((2, PATCHES)),
            dma((2,)),
            dma((2,)),
            dma(()),
            dma(()),
        ],
        compiler_params=pltpu.CompilerParams(
            collective_id=0, has_side_effects=True, vmem_limit_bytes=63 * 1024 * 1024
        ),
        name="pipeline",
    )(
        order, step_index, pattern,
        hidden.reshape(PATCHES, ROWS, D), stale_kv.reshape(PATCHES, ROWS, 2 * INNER), w_qkv[0], w_out[0],
        q_gain, k_gain, mod_table.reshape(TSTEPS * 3, D),
    )

    def slot_of(patch, order_ref):
        slot = jnp.int32(0)
        for index in range(1, PATCHES):
            slot = jnp.where(order_ref[index] == patch, index, slot)
        return (slot, 0, 0)

    layer_out, kv_cache = pl.pallas_call(
        to_patch_order,
        out_shape=(
            jax.ShapeDtypeStruct((PATCHES, ROWS, D), bf16),
            jax.ShapeDtypeStruct((PATCHES, ROWS, 2 * INNER), bf16),
        ),
        grid_spec=pltpu.PrefetchScalarGridSpec(
            num_scalar_prefetch=1,
            grid=(PATCHES,),
            in_specs=[pl.BlockSpec((1, ROWS, D), slot_of), pl.BlockSpec((1, ROWS, 2 * INNER), slot_of)],
            out_specs=[
                pl.BlockSpec((1, ROWS, D), lambda patch, order_ref: (patch, 0, 0)),
                pl.BlockSpec((1, ROWS, 2 * INNER), lambda patch, order_ref: (patch, 0, 0)),
            ],
        ),
        name="patch_order",
    )(order, rows_slots, kv_slots)
    return (layer_out.reshape(1, SEQ_DEV, D), kv_cache.reshape(1, SEQ_DEV, 2 * INNER))


def solution(mesh):
    in_specs = (
        P("blk", None),
        P("section", "blk", None),
        P("section", "blk", None),
        P("section", "blk", None),
        P("section", None),
        P("section", None),
        P("section", None, None, None),
        P("blk", None),
        P("blk"),
        P(),
    )
    out_specs = (P("section", "blk", None), P("section", "blk", None))
    return jax.shard_map(
        on_device, mesh=mesh, in_specs=in_specs, out_specs=out_specs, check_vma=False
    )
```

time: 1030 us -> 396 us (0.38); the launches traced: 1010 us -> 393 us
  waiting for transfers between devices: 636 us -> 0 us
  Pallas kernels: 0 us -> 390 us
  other arithmetic: 126 us -> 0 us
  local copies, waits for them, and re-layouts: 103 us -> 2.03 us
  matrix products: 82.5 us -> 0 us
  starting transfers between devices: 32.5 us -> 0 us
  loops' own time: 20.9 us -> 0 us
  between operations: 14.1 us -> 0.64 us
    ppermute x23 -> x0, waiting for transfers between devices: 505 us -> none  [the longest x11 284 us: shifted_2(): return lax.ppermute(x, axis, pairs)]
    pallas_call x0 -> x2, Pallas kernels: none -> 390 us  [the longest x1 385 us: on_device(): pl.pallas_call(kernel, out_shape=(jax.ShapeDtypeStruct((PATCHES, ROWS, D)...]
    all_gather x2 -> x0, waiting for transfers between devices: 130 us -> none  [the longest x1 130 us: on_device(): lax.all_gather(w_qkv[0], 'blk', axis=0, tiled=True)]
    dot_general x27 -> x0, matrix products: 82.5 us -> none  [the longest x4 28.6 us: project(): qkv = jnp.dot(modulated, full_qkv, preferred_element_type=jnp.float32)]
    select_n x44 -> x0, other arithmetic: 81.4 us -> none  [the longest x11 25.1 us: slot_step(): jnp.where(active, lax.dynamic_update_index_in_dim(own_store, fresh_kv, pa...]
    ppermute x23 -> x0, starting transfers between devices: 32.4 us -> none  [the longest x12 18.3 us: shifted(): return lax.ppermute(value, axis, pairs)]
    reshape x8 -> x1, local copies, waits for them, and re-layouts: 31.6 us -> 0.86 us  [on_device(): mod_table.reshape(TSTEPS * 3, D)]
    concatenate x4 -> x0, other arithmetic: 22.5 us -> none  [attend(): jnp.concatenate([own_rows.reshape(-1, 2 * inner_width), near_rows.reshape...]
  transfers between devices with their start and end apart: 25 -> 0, of which waited for: 25 -> 0; matrix products, arithmetic and copies ran while one was open for 5% -> 0% of each run, Pallas kernels for 0% -> 0%
where the time goes in v1:
time: 396 us; the launch traced here: 393 us
  Pallas kernels  390 us (98%)
    pallas_call x1, Pallas kernels, on_device(): pl.pallas_call(kernel, out_shape=(jax.ShapeDtypeStruct((PATCHES, ROWS, D)...  385 us

profile of v1, /device:TPU:103, one launch (start us, length us, event | category | flops | bytes accessed | tf_op | source)
XLA Modules:
  0.0 393.0 jit_solution(17354990249731176472)
XLA Ops:
  0.6 1.2 copy.13
  1.8 0.9 reshape.21.mod_table
  2.7 384.6 %pipeline.1 = (bf16[4,128,1536]{2,1,0:T(8,128)(2,1)}, bf16[4,128,3072]{2,1,0:T(8,128)(2,1)}) custom-call(s32[4]{0:T(128)} %order_s.3, s32[4]{0:T(128)} %step_s.1, s32[4,8]{1,0:T(4,128)} %pattern_s.1, bf16[4,128,1536]{2,1,0:T(8,128)(2,1)} %bitcast.7, bf16[4,128,3072]{2,1,0:T(8,128)(2,1)} %bitcast.6, bf16[48,4608]{1,0:T(8,128)(2,1)} %bitcast.8, ...), custom_call_target="tpu_custom_call" | custom-call | tf_op jit(solution)/shard_map/pipeline/pallas_call | solution.py:339
  387.3 5.7 %patch_order.1 = (bf16[4,128,1536]{2,1,0:T(8,128)(2,1)}, bf16[4,128,3072]{2,1,0:T(8,128)(2,1)}) custom-call(s32[4]{0:T(128)} %order_s.3, bf16[4,128,1536]{2,1,0:T(8,128)(2,1)} %get-tuple-element.6.rows_in, bf16[4,128,3072]{2,1,0:T(8,128)(2,1)} %get-tuple-element.7.kv_in), custom_call_target="tpu_custom_call" | custom-call | tf_op jit(solution)/shard_map/patch_order/pallas_call | solution.py:393

commit v2 on v1

--- a/solution.py
+++ b/solution.py
@@ -22,8 +22,12 @@
 NSEC = 8
 SHARD = D // NBLK
 NORM_EPS = 1e-06
-CHUNK = 512
-N_SEND = 70
+CHUNK = 768
+SPLIT_QKV, SPLIT_OUT = 2560, 1024
+OFFSETS = (0, 1, -1, 2, -2, 3, 4, 5)
+FAR_UP, FAR_DOWN = 5, 2
+HELPED = 2
+HELPERS = NSEC - HELPED
 SCORE_SCALE = math.log2(math.e) / math.sqrt(HDIM)
 
 
@@ -42,8 +46,8 @@
 def kernel(
     order_s, step_s, pattern_s, hidden_h, stale_h, wq_h, wo_h, qgain, kgain, mod_table,
     out_h, kv_h,
-    wq, wo, keys, values, x_own, x_near, mod_own, mod_near, stale, hidden, fresh, out_rows, modulated, queries, attended,
-    recv_q, recv_o, send, local, rx_own, rx_near, tx_own, tx_near, store_sem, rx_stale, tx_stale, rx_mod, tx_mod,
+    wq, wo, wo_help, keys, values, x_own, x_near, mod_own, mod_near, stale, hidden, fresh, out_rows, modulated, queries, attended,
+    recv_a, recv_b, recv_o, recv_p, recv_h, send_a, send_b, send_o, send_p, send_h, send_x, local, rx_own, rx_near, tx_own, tx_near, store_sem, rx_stale, tx_stale, rx_mod, tx_mod,
 ):
     sec = lax.axis_index("section")
     blk = lax.axis_index("blk")
@@ -54,6 +58,7 @@
 
     up, down = lax.rem(sec + 1, NSEC), lax.rem(sec + NSEC - 1, NSEC)
     after, before = lax.rem(blk + 1, NBLK), lax.rem(blk + NBLK - 1, NBLK)
+    chip_up, chip_down = lax.rem(sec + 2, NSEC), lax.rem(sec + NSEC - 2, NSEC)
     zp, zm, yp, ym = at(y, z + 1), at(y, z - 1), at(y + 1, z), at(y - 1, z)
 
     load_hidden = pltpu.make_async_copy(hidden_h, hidden, local.at[0])
@@ -68,48 +73,137 @@
     barrier = pltpu.get_barrier_semaphore()
     for target in (
         (sec, zp), (sec, zm), (sec, yp), (sec, ym), (sec, after), (sec, before),
-        (up, blk), (down, blk), (up, after), (down, before),
+        (up, blk), (down, blk), (up, after), (down, before), (chip_up, blk), (chip_down, blk),
     ):
         pl.semaphore_signal(barrier, inc=1, device_id=target, device_id_type=MESH)
-    pl.semaphore_wait(barrier, 10)
-
-    sends = []
-
-    def push(which, shard, target, source=None):
-        buffer, recv = (wq, recv_q) if which == "q" else (wo, recv_o)
-        rows = buffer.at[pl.ds(shard * SHARD, SHARD)]
-        copy = pltpu.make_async_remote_copy(
-            src_ref=rows if source is None else source,
-            dst_ref=rows,
-            send_sem=send.at[len(sends)],
-            recv_sem=recv.at[shard],
-            device_id=(sec, target),
-            device_id_type=MESH,
-        )
-        copy.start()
-        sends.append(copy)
-
-    def arrived(which, shard):
-        buffer, recv = (wq, recv_q) if which == "q" else (wo, recv_o)
-        rows = buffer.at[pl.ds(shard * SHARD, SHARD)]
-        pltpu.make_async_remote_copy(
-            src_ref=rows, dst_ref=rows, send_sem=send.at[0], recv_sem=recv.at[shard],
-            device_id=(sec, blk), device_id_type=MESH,
-        ).wait_recv()
-
-    push("o", blk, yp, wo_h)
-    push("o", blk, ym, wo_h)
-    push("q", blk, zp, wq_h)
-    push("q", blk, zm, wq_h)
-    push("q", blk, yp, wq_h)
-    push("q", blk, ym, wq_h)
-    push("o", blk, zp, wo_h)
-    push("o", blk, zm, wo_h)
+    pl.semaphore_wait(barrier, 12)
+
+
+    class Gather:
+        def __init__(self, buffer, start, stop, recv, send, source):
+            self.buffer, self.columns = buffer, pl.ds(start, stop - start)
+            self.recv, self.send, self.source = recv, send, source
+            self.count = 0
+
+        def rows(self, shard):
+            return self.buffer.at[pl.ds(pl.multiple_of(shard * SHARD, 16), SHARD), self.columns]
+
+        def push(self, shard, *targets, from_input=False, to=None):
+            for target in targets:
+                copy = pltpu.make_async_remote_copy(
+                    src_ref=self.source.at[:, self.columns] if from_input else self.rows(shard),
+                    dst_ref=(self if to is None else to).rows(shard),
+                    send_sem=self.send.at[self.count],
+                    recv_sem=(self if to is None else to).recv.at[shard],
+                    device_id=target if isinstance(target, tuple) else (sec, target),
+                    device_id_type=MESH,
+                )
+                copy.start()
+                self.count += 1
+
+        def arrived(self, shard):
+            pltpu.make_async_remote_copy(
+                src_ref=self.rows(shard), dst_ref=self.rows(shard), send_sem=self.send.at[0],
+                recv_sem=self.recv.at[shard], device_id=(up, blk), device_id_type=MESH,
+            ).wait_recv()
+
+        def along(self, shard, k):
+            if OFFSETS[k] == 0:
+                self.push(shard, zp, zm)
+            elif 0 < OFFSETS[k] < FAR_UP:
+                self.push(shard, zm)
+            elif -FAR_DOWN < OFFSETS[k] < 0:
+                self.push(shard, zp)
+
+        def cross(self, k, level):
+            zk = z + OFFSETS[k]
+            here, there = at(y - 1, zk), at(y + 1, zk)
+            self.arrived(here)
+            self.arrived(there)
+            if level:
+                odd = lax.rem(zk + 2 * NZ, 2) == 1
+                self.push(jnp.where(odd, there, here), jnp.where(odd, ym, yp))
+            else:
+                self.push(there, ym)
+            return here, there
+
+        def wait_sends(self):
+            for index in range(self.count):
+                pltpu.make_async_remote_copy(
+                    src_ref=self.rows(blk), dst_ref=self.rows(blk), send_sem=self.send.at[index],
+                    recv_sem=self.recv.at[blk], device_id=(up, blk), device_id_type=MESH,
+                ).wait_send()
+
+    def gather(main, side, level, extras=()):
+        side.arrived(ym)
+        side.arrived(yp)
+        if level:
+            even = lax.rem(z, 2) == 0
+            side.push(jnp.where(even, ym, yp), jnp.where(even, yp, ym))
+        else:
+            side.push(yp, ym)
+        side.push(ym, zp, zm)
+        side.push(yp, zp, zm)
+        for k in range(1, NZ):
+            shard = at(y, z + OFFSETS[k])
+            main.arrived(shard)
+            main.along(shard, k)
+            main.push(shard, yp, ym)
+            if k == 1:
+                side.arrived(at(y + 2, z))
+                side.push(at(y + 2, z), zp, zm)
+            main.cross(k - 1, level)
+            for i in range(NY):
+                shard = at(y + i, z + OFFSETS[k])
+                side.arrived(shard)
+                side.along(shard, k)
+            if k - 1 < len(extras):
+                extras[k - 1].start()
+        main.cross(NZ - 1, level)
+        for k in range(NZ):
+            main.arrived(at(y + 2, z + OFFSETS[k]))
+
+    qkv_main = Gather(wq, 0, SPLIT_QKV, recv_a, send_a, wq_h)
+    qkv_side = Gather(wq, SPLIT_QKV, 3 * INNER, recv_b, send_b, wq_h)
+    out_main = Gather(wo, 0, SPLIT_OUT, recv_o, send_o, wo_h)
+    out_side = Gather(wo, SPLIT_OUT, D, recv_p, send_p, wo_h)
+    help_out = Gather(wo_help, 0, D, recv_h, send_h, wo_h)
+    helped_out = Gather(wo, 0, D, recv_o, send_x, wo_h)
+
+    @pl.when(sec < HELPED)
+    def _():
+        helped_out.push(blk, (chip_down, blk), from_input=True, to=help_out)
+
+    @pl.when(sec >= HELPERS)
+    def _():
+        for k in range(NZ):
+            shard = at(y, z + OFFSETS[k])
+            help_out.arrived(shard)
+            help_out.along(shard, k)
+            help_out.push(shard, yp, ym)
+            if k > 0:
+                help_out.push(shard, (chip_up, blk), to=helped_out)
+                for shard in help_out.cross(k - 1, True):
+                    help_out.push(shard, (chip_up, blk), to=helped_out)
+            if k > 1:
+                shard = at(y + 2, z + OFFSETS[k - 2])
+                help_out.arrived(shard)
+                help_out.push(shard, (chip_up, blk), to=helped_out)
+        for shard in help_out.cross(NZ - 1, True):
+            help_out.push(shard, (chip_up, blk), to=helped_out)
+        for k in (NZ - 2, NZ - 1):
+            shard = at(y + 2, z + OFFSETS[k])
+            help_out.arrived(shard)
+            help_out.push(shard, (chip_up, blk), to=helped_out)
+
+    qkv_side.push(blk, yp, ym, from_input=True)
+    qkv_main.push(blk, zp, zm, yp, ym, from_input=True)
+    qkv_side.push(blk, zp, zm, from_input=True)
 
     for slot in range(PATCHES):
         step = step_s[order_s[slot]]
         for row in range(3):
-            mod_own[slot, pl.ds(row, 1), :] = mod_table[pl.ds(3 * step + row, 1), :]
+            mod_own[pl.ds(4 * slot + row, 1), :] = mod_table[pl.ds(3 * step + row, 1), :]
     send_mod = pltpu.make_async_remote_copy(
         src_ref=mod_own, dst_ref=mod_near, send_sem=tx_mod, recv_sem=rx_mod,
         device_id=(sec, after), device_id_type=MESH,
@@ -128,8 +222,7 @@
     def _():
         for slot in range(PATCHES):
             x_own[slot] = hidden[order_s[slot]]
-        for slot in range(PATCHES):
-            near_copy(slot).start()
+        near_copy(0).start()
 
     load_stale.wait()
     for slot in range(1, PATCHES):
@@ -140,60 +233,34 @@
                 stale[patch, :, columns].astype(jnp.float32), kgain[...]
             ).astype(jnp.bfloat16)
         values[pl.ds(slot * ROWS, ROWS), :] = stale[patch, :, INNER:]
-    stale_sends = []
-    for index, buffer in enumerate((keys, values)):
-        copy = pltpu.make_async_remote_copy(
-            src_ref=buffer.at[pl.ds(ROWS, SEQ_DEV - ROWS)],
-            dst_ref=buffer.at[pl.ds(SEQ_DEV + ROWS, SEQ_DEV - ROWS)],
-            send_sem=tx_stale.at[index], recv_sem=rx_stale.at[index],
-            device_id=(sec, after), device_id_type=MESH,
-        )
-        copy.start()
-        stale_sends.append(copy)
-
-    even = lax.rem(z, 2) == 0
-    arrived("o", ym)
-    arrived("o", yp)
-    push("o", jnp.where(even, ym, yp), jnp.where(even, yp, ym))
-    for shard in (ym, yp):
-        push("o", shard, zp)
-        push("o", shard, zm)
-    arrived("o", at(y + 2, z))
-    push("o", at(y + 2, z), zp)
-    push("o", at(y + 2, z), zm)
-
-    def cross(zk):
-        arrived("q", at(y - 1, zk))
-        arrived("q", at(y + 1, zk))
-        odd = lax.rem(zk + NZ, 2) == 1
-        push("q", jnp.where(odd, at(y + 1, zk), at(y - 1, zk)), jnp.where(odd, ym, yp))
-
-    previous = z
-    for k in range(1, NZ):
-        if k == NZ - 1:
-            zk, forward = z + NZ // 2, None
-        elif k % 2 == 1:
-            zk, forward = z - (k + 1) // 2, (zp if k < NZ - 3 else None)
-        else:
-            zk, forward = z + k // 2, zm
-        arrived("q", at(y, zk))
-        if forward is not None:
-            push("q", at(y, zk), forward)
-        push("q", at(y, zk), yp)
-        push("q", at(y, zk), ym)
-        cross(previous)
-        for i in range(NY):
-            arrived("o", at(y + i, zk))
-            if forward is not None:
-                push("o", at(y + i, zk), forward)
-        previous = zk
-    cross(previous)
-    for i in range(NZ):
-        arrived("q", at(y + 2, z + i))
+    stale_copies = []
+    for slot in range(1, PATCHES):
+        for index, buffer in enumerate((keys, values)):
+            stale_copies.append(pltpu.make_async_remote_copy(
+                src_ref=buffer.at[pl.ds(slot * ROWS, ROWS)],
+                dst_ref=buffer.at[pl.ds(SEQ_DEV + slot * ROWS, ROWS)],
+                send_sem=tx_stale.at[index, slot], recv_sem=rx_stale.at[index, slot],
+                device_id=(sec, after), device_id_type=MESH,
+            ))
+
+    gather(qkv_main, qkv_side, False, stale_copies)
+
+    @pl.when(sec == 0)
+    def _():
+        for slot in range(1, PATCHES):
+            near_copy(slot).start()
+
+    @pl.when(sec >= HELPED)
+    def _():
+        out_side.push(blk, yp, ym, from_input=True)
+        out_main.push(blk, zp, zm, yp, ym, from_input=True)
+        out_side.push(blk, zp, zm, from_input=True)
+        gather(out_main, out_side, True)
+
     load_wq.wait()
     load_wo.wait()
     send_mod.wait()
-    for copy in stale_sends:
+    for copy in stale_copies:
         copy.wait()
 
     def slot_step(slot, carry):
@@ -205,11 +272,11 @@
             ).wait_recv()
 
         modulated[pl.ds(0, ROWS), :] = modulate(
-            x_own[slot], mod_own[slot, pl.ds(1, 1), :], mod_own[slot, pl.ds(0, 1), :]
+            x_own[slot], mod_own[pl.ds(4 * slot + 1, 1), :], mod_own[pl.ds(4 * slot, 1), :]
         )
         near_copy(slot).wait_recv()
         modulated[pl.ds(ROWS, ROWS), :] = modulate(
-            x_near[slot], mod_near[slot, pl.ds(1, 1), :], mod_near[slot, pl.ds(0, 1), :]
+            x_near[slot], mod_near[pl.ds(4 * slot + 1, 1), :], mod_near[pl.ds(4 * slot, 1), :]
         )
         own_rows = pl.ds(pl.multiple_of(slot * ROWS, ROWS), ROWS)
         near_rows = pl.ds(pl.multiple_of(SEQ_DEV + slot * ROWS, ROWS), ROWS)
@@ -277,15 +344,20 @@
             attended[:, columns] = (mixture / weight_sum).astype(jnp.bfloat16)
             return carry
 
-        lax.fori_loop(0, HEADS, attend, 0, unroll=2)
+        lax.fori_loop(0, HEADS, attend, 0, unroll=4)
 
         def project_out(chunk, carry):
             columns = pl.ds(pl.multiple_of(chunk * CHUNK, CHUNK), CHUNK)
             product = jnp.dot(attended[...], wo[:, columns], preferred_element_type=jnp.float32)
             out_rows[slot, :, columns] = (
-                x_own[slot, :, columns].astype(jnp.float32) + mod_own[slot, pl.ds(2, 1), columns] * product
+                x_own[slot, :, columns].astype(jnp.float32) + mod_own[pl.ds(4 * slot + 2, 1), columns] * product
             ).astype(jnp.bfloat16)
             return carry
+
+        @pl.when(jnp.logical_and(sec < HELPED, slot == 0))
+        def _():
+            for i in range(NBLK - 1):
+                helped_out.arrived(lax.rem(blk + 1 + i, NBLK))
 
         lax.fori_loop(0, D // CHUNK, project_out, 0)
 
@@ -307,8 +379,17 @@
 
     lax.fori_loop(0, PATCHES, slot_step, 0)
 
-    for copy in sends:
-        copy.wait_send()
+    qkv_main.wait_sends()
+    qkv_side.wait_sends()
+
+    @pl.when(sec >= HELPED)
+    def _():
+        out_main.wait_sends()
+        out_side.wait_sends()
+
+    pl.when(sec >= HELPERS)(help_out.wait_sends)
+    pl.when(sec < HELPED)(helped_out.wait_sends)
+
     for slot in range(PATCHES):
         pltpu.make_async_copy(fresh.at[slot], kv_h.at[slot], store_sem.at[0, slot]).wait()
         pltpu.make_async_copy(out_rows.at[slot], out_h.at[slot], store_sem.at[1, slot]).wait()
@@ -347,12 +428,13 @@
         scratch_shapes=[
             pltpu.VMEM((D, 3 * INNER), bf16),
             pltpu.VMEM((INNER, D), bf16),
+            pltpu.VMEM((INNER, D), bf16),
             pltpu.VMEM((2 * SEQ_DEV, INNER), bf16),
             pltpu.VMEM((2 * SEQ_DEV, INNER), bf16),
             pltpu.VMEM((PATCHES, ROWS, D), bf16),
             pltpu.VMEM((PATCHES, ROWS, D), bf16),
-            pltpu.VMEM((PATCHES, 8, D), f32),
-            pltpu.VMEM((PATCHES, 8, D), f32),
+            pltpu.VMEM((4 * PATCHES, D), f32),
+            pltpu.VMEM((4 * PATCHES, D), f32),
             pltpu.VMEM((PATCHES, ROWS, 2 * INNER), bf16),
             pltpu.VMEM((PATCHES, ROWS, D), bf16),
             pltpu.VMEM((PATCHES, ROWS, 2 * INNER), bf16),
@@ -362,15 +444,23 @@
             pltpu.VMEM((ROWS, INNER), bf16),
             dma((NBLK,)),
             dma((NBLK,)),
-            dma((N_SEND,)),
+            dma((NBLK,)),
+            dma((NBLK,)),
+            dma((NBLK,)),
+            dma((31,)),
+            dma((31,)),
+            dma((31,)),
+            dma((31,)),
+            dma((62,)),
+            dma((1,)),
             dma((4,)),
             dma((PATCHES,)),
             dma((PATCHES,)),
             dma((PATCHES,)),
             dma((PATCHES,)),
             dma((2, PATCHES)),
-            dma((2,)),
-            dma((2,)),
+            dma((2, PATCHES)),
+            dma((2, PATCHES)),
             dma(()),
             dma(()),
         ],

time: 396 us -> 332 us (0.84)
  Pallas kernels: 390 us -> 329 us
    pallas_call x1, Pallas kernels: 385 us -> 323 us  [on_device(): pl.pallas_call(kernel, out_shape=(jax.ShapeDtypeStruct((PATCHES, ROWS, D)...]
where the time goes in v2:
time: 332 us; the launch traced here: 331 us
  Pallas kernels  329 us (99%)
    pallas_call x1, Pallas kernels, on_device(): pl.pallas_call(kernel, out_shape=(jax.ShapeDtypeStruct((PATCHES, ROWS, D)...  323 us

profile of v2, /device:TPU:103, one launch (start us, length us, event | category | flops | bytes accessed | tf_op | source)
XLA Modules:
  0.0 331.3 jit_solution(131902300300920223)
XLA Ops:
  0.6 1.2 copy.13
  1.8 0.9 reshape.21.mod_table
  2.7 323.0 %pipeline.1 = (bf16[4,128,1536]{2,1,0:T(8,128)(2,1)}, bf16[4,128,3072]{2,1,0:T(8,128)(2,1)}) custom-call(s32[4]{0:T(128)} %order_s.3, s32[4]{0:T(128)} %step_s.1, s32[4,8]{1,0:T(4,128)} %pattern_s.1, bf16[4,128,1536]{2,1,0:T(8,128)(2,1)} %bitcast.7, bf16[4,128,3072]{2,1,0:T(8,128)(2,1)} %bitcast.6, bf16[48,4608]{1,0:T(8,128)(2,1)} %bitcast.8, ...), custom_call_target="tpu_custom_call" | custom-call | tf_op jit(solution)/shard_map/pipeline/pallas_call | solution.py:420
  325.6 5.7 %patch_order.1 = (bf16[4,128,1536]{2,1,0:T(8,128)(2,1)}, bf16[4,128,3072]{2,1,0:T(8,128)(2,1)}) custom-call(s32[4]{0:T(128)} %order_s.3, bf16[4,128,1536]{2,1,0:T(8,128)(2,1)} %get-tuple-element.6.rows_in, bf16[4,128,3072]{2,1,0:T(8,128)(2,1)} %get-tuple-element.7.kv_in), custom_call_target="tpu_custom_call" | custom-call | tf_op jit(solution)/shard_map/patch_order/pallas_call | solution.py:483

commit v3 on v2

--- a/solution.py
+++ b/solution.py
@@ -23,9 +23,11 @@
 SHARD = D // NBLK
 NORM_EPS = 1e-06
 CHUNK = 768
+CHUNKS = INNER // CHUNK
 SPLIT_QKV, SPLIT_OUT = 2560, 1024
 OFFSETS = (0, 1, -1, 2, -2, 3, 4, 5)
 FAR_UP, FAR_DOWN = 5, 2
+PARTWAY = 2
 HELPED = 2
 HELPERS = NSEC - HELPED
 SCORE_SCALE = math.log2(math.e) / math.sqrt(HDIM)
@@ -46,8 +48,8 @@
 def kernel(
     order_s, step_s, pattern_s, hidden_h, stale_h, wq_h, wo_h, qgain, kgain, mod_table,
     out_h, kv_h,
-    wq, wo, wo_help, keys, values, x_own, x_near, mod_own, mod_near, stale, hidden, fresh, out_rows, modulated, queries, attended,
-    recv_a, recv_b, recv_o, recv_p, recv_h, send_a, send_b, send_o, send_p, send_h, send_x, local, rx_own, rx_near, tx_own, tx_near, store_sem, rx_stale, tx_stale, rx_mod, tx_mod,
+    wq, wo, wo_help, keys, values, x_own, x_near, mod_own, mod_near, stale, hidden, fresh, out_rows, modulated, queries, attended, relay,
+    recv_a, recv_b, recv_o, recv_p, recv_h, send_a, send_b, send_o, send_p, send_h, send_x, local, rx_own, rx_near, tx_own, tx_near, tx_next, go, store_sem, rx_stale, tx_stale, rx_relay, tx_relay, rx_mod, tx_mod,
 ):
     sec = lax.axis_index("section")
     blk = lax.axis_index("blk")
@@ -134,7 +136,7 @@
                     recv_sem=self.recv.at[blk], device_id=(up, blk), device_id_type=MESH,
                 ).wait_send()
 
-    def gather(main, side, level, extras=()):
+    def gather(main, side, level, between=lambda k: None):
         side.arrived(ym)
         side.arrived(yp)
         if level:
@@ -157,8 +159,7 @@
                 shard = at(y + i, z + OFFSETS[k])
                 side.arrived(shard)
                 side.along(shard, k)
-            if k - 1 < len(extras):
-                extras[k - 1].start()
+            between(k)
         main.cross(NZ - 1, level)
         for k in range(NZ):
             main.arrived(at(y + 2, z + OFFSETS[k]))
@@ -173,6 +174,15 @@
     @pl.when(sec < HELPED)
     def _():
         helped_out.push(blk, (chip_down, blk), from_input=True, to=help_out)
+
+    is_even = lax.rem(sec, 2) == 0
+
+    def let_go():
+        pl.semaphore_signal(go, inc=1, device_id=(up, blk), device_id_type=MESH)
+
+    @pl.when(jnp.logical_not(is_even))
+    def _():
+        pl.semaphore_wait(go, 1)
 
     @pl.when(sec >= HELPERS)
     def _():
@@ -196,6 +206,7 @@
             help_out.arrived(shard)
             help_out.push(shard, (chip_up, blk), to=helped_out)
 
+    pl.when(sec == HELPERS)(let_go)
     qkv_side.push(blk, yp, ym, from_input=True)
     qkv_main.push(blk, zp, zm, yp, ym, from_input=True)
     qkv_side.push(blk, zp, zm, from_input=True)
@@ -212,17 +223,29 @@
 
     load_hidden.wait()
 
-    def near_copy(slot):
+    def near_copy(slot, chunk):
+        columns = pl.ds(chunk * CHUNK, CHUNK)
         return pltpu.make_async_remote_copy(
-            src_ref=x_own.at[slot], dst_ref=x_near.at[slot], send_sem=tx_near.at[slot], recv_sem=rx_near.at[slot],
+            src_ref=x_own.at[slot, :, columns], dst_ref=x_near.at[slot, :, columns],
+            send_sem=tx_near.at[slot, chunk], recv_sem=rx_near.at[slot, chunk],
             device_id=(sec, after), device_id_type=MESH,
         )
 
+    def next_copy(slot, chunk, near):
+        columns = pl.ds(pl.multiple_of(chunk * CHUNK, CHUNK), CHUNK)
+        landing, tx, rx, target = (x_near, tx_next, rx_near, after) if near else (x_own, tx_own, rx_own, blk)
+        return pltpu.make_async_remote_copy(
+            src_ref=out_rows.at[slot, :, columns], dst_ref=landing.at[slot, :, columns],
+            send_sem=tx.at[slot, chunk], recv_sem=rx.at[slot, chunk],
+            device_id=(up, target), device_id_type=MESH,
+        )
+
     @pl.when(sec == 0)
     def _():
         for slot in range(PATCHES):
             x_own[slot] = hidden[order_s[slot]]
-        near_copy(0).start()
+        for chunk in range(CHUNKS):
+            near_copy(0, chunk).start()
 
     load_stale.wait()
     for slot in range(1, PATCHES):
@@ -233,22 +256,55 @@
                 stale[patch, :, columns].astype(jnp.float32), kgain[...]
             ).astype(jnp.bfloat16)
         values[pl.ds(slot * ROWS, ROWS), :] = stale[patch, :, INNER:]
-    stale_copies = []
-    for slot in range(1, PATCHES):
-        for index, buffer in enumerate((keys, values)):
-            stale_copies.append(pltpu.make_async_remote_copy(
-                src_ref=buffer.at[pl.ds(slot * ROWS, ROWS)],
-                dst_ref=buffer.at[pl.ds(SEQ_DEV + slot * ROWS, ROWS)],
-                send_sem=tx_stale.at[index, slot], recv_sem=rx_stale.at[index, slot],
-                device_id=(sec, after), device_id_type=MESH,
-            ))
-
-    gather(qkv_main, qkv_side, False, stale_copies)
+    pieces = 2 * (PATCHES - 1)
+    by_relay = jnp.logical_and(jnp.logical_not(is_even), z == NZ - 1)
+
+    def stale_rows(i, half):
+        buffer = (keys, values)[i % 2]
+        return buffer.at[pl.ds(half * SEQ_DEV + (i // 2 + 1) * ROWS, ROWS)]
+
+    def stale_copy(i):
+        return pltpu.make_async_remote_copy(
+            src_ref=stale_rows(i, 0), dst_ref=stale_rows(i, 1), send_sem=tx_stale.at[i], recv_sem=rx_stale.at[i],
+            device_id=(sec, after), device_id_type=MESH,
+        )
+
+    def relay_copy(i, second):
+        return pltpu.make_async_remote_copy(
+            src_ref=relay.at[i] if second else stale_rows(i, 0),
+            dst_ref=stale_rows(i, 1) if second else relay.at[i],
+            send_sem=(tx_relay if second else tx_stale).at[i],
+            recv_sem=(rx_stale if second else rx_relay).at[i],
+            device_id=(sec, zp if second else yp), device_id_type=MESH,
+        )
+
+    def between(k):
+        if 1 <= k <= pieces:
+            @pl.when(by_relay)
+            def _():
+                relay_copy(k - 1, False).start()
+
+            @pl.when(jnp.logical_not(by_relay))
+            def _():
+                stale_copy(k - 1).start()
+
+        if 3 <= k < pieces + 3:
+            @pl.when(by_relay)
+            def _():
+                relay_copy(k - 3, False).wait_recv()
+                relay_copy(k - 3, True).start()
+
+        if k == PARTWAY:
+            pl.when(jnp.logical_and(is_even, sec < HELPERS))(let_go)
+
+    gather(qkv_main, qkv_side, False, between)
+    between(NZ)
 
     @pl.when(sec == 0)
     def _():
         for slot in range(1, PATCHES):
-            near_copy(slot).start()
+            for chunk in range(CHUNKS):
+                near_copy(slot, chunk).start()
 
     @pl.when(sec >= HELPED)
     def _():
@@ -260,23 +316,26 @@
     load_wq.wait()
     load_wo.wait()
     send_mod.wait()
-    for copy in stale_copies:
-        copy.wait()
+    for i in range(pieces):
+        stale_copy(i).wait()
+
+    @pl.when(by_relay)
+    def _():
+        for i in range(pieces):
+            relay_copy(i, True).wait_send()
 
     def slot_step(slot, carry):
         @pl.when(sec > 0)
         def _():
-            pltpu.make_async_remote_copy(
-                src_ref=x_own.at[slot], dst_ref=x_own.at[slot], send_sem=tx_own.at[slot], recv_sem=rx_own.at[slot],
-                device_id=(up, blk), device_id_type=MESH,
-            ).wait_recv()
+            for chunk in range(CHUNKS):
+                next_copy(slot, chunk, False).wait_recv()
+
+                @pl.when(is_even)
+                def _():
+                    near_copy(slot, chunk).start()
 
         modulated[pl.ds(0, ROWS), :] = modulate(
             x_own[slot], mod_own[pl.ds(4 * slot + 1, 1), :], mod_own[pl.ds(4 * slot, 1), :]
-        )
-        near_copy(slot).wait_recv()
-        modulated[pl.ds(ROWS, ROWS), :] = modulate(
-            x_near[slot], mod_near[pl.ds(4 * slot + 1, 1), :], mod_near[pl.ds(4 * slot, 1), :]
         )
         own_rows = pl.ds(pl.multiple_of(slot * ROWS, ROWS), ROWS)
         near_rows = pl.ds(pl.multiple_of(SEQ_DEV + slot * ROWS, ROWS), ROWS)
@@ -317,9 +376,14 @@
             values[near_rows, pl.ds(base, CHUNK)] = product[ROWS:]
             return carry
 
-        lax.fori_loop(0, INNER // CHUNK, project_q, 0)
-        lax.fori_loop(0, INNER // CHUNK, project_k, 0)
-        lax.fori_loop(0, INNER // CHUNK, project_v, 0)
+        lax.fori_loop(0, CHUNKS, project_q, 0)
+        for chunk in range(CHUNKS):
+            near_copy(slot, chunk).wait_recv()
+        modulated[pl.ds(ROWS, ROWS), :] = modulate(
+            x_near[slot], mod_near[pl.ds(4 * slot + 1, 1), :], mod_near[pl.ds(4 * slot, 1), :]
+        )
+        lax.fori_loop(0, CHUNKS, project_k, 0)
+        lax.fori_loop(0, CHUNKS, project_v, 0)
         pltpu.make_async_copy(fresh.at[slot], kv_h.at[slot], store_sem.at[0, slot]).start()
 
         patch = order_s[slot]
@@ -352,6 +416,15 @@
             out_rows[slot, :, columns] = (
                 x_own[slot, :, columns].astype(jnp.float32) + mod_own[pl.ds(4 * slot + 2, 1), columns] * product
             ).astype(jnp.bfloat16)
+
+            @pl.when(sec < NSEC - 1)
+            def _():
+                next_copy(slot, chunk, False).start()
+
+                @pl.when(is_even)
+                def _():
+                    next_copy(slot, chunk, True).start()
+
             return carry
 
         @pl.when(jnp.logical_and(sec < HELPED, slot == 0))
@@ -359,23 +432,10 @@
             for i in range(NBLK - 1):
                 helped_out.arrived(lax.rem(blk + 1 + i, NBLK))
 
-        lax.fori_loop(0, D // CHUNK, project_out, 0)
-
-        @pl.when(sec < NSEC - 1)
-        def _():
-            for target, landing, tx, rx in ((blk, x_own, tx_own, rx_own), (after, x_near, tx_near, rx_near)):
-                pltpu.make_async_remote_copy(
-                    src_ref=out_rows.at[slot], dst_ref=landing.at[slot], send_sem=tx.at[slot], recv_sem=rx.at[slot],
-                    device_id=(up, target), device_id_type=MESH,
-                ).start()
+        lax.fori_loop(0, CHUNKS, project_out, 0)
 
         pltpu.make_async_copy(out_rows.at[slot], out_h.at[slot], store_sem.at[1, slot]).start()
         return carry
-
-    @pl.when(sec == 0)
-    def _():
-        for slot in range(PATCHES):
-            near_copy(slot).wait_send()
 
     lax.fori_loop(0, PATCHES, slot_step, 0)
 
@@ -394,14 +454,18 @@
         pltpu.make_async_copy(fresh.at[slot], kv_h.at[slot], store_sem.at[0, slot]).wait()
         pltpu.make_async_copy(out_rows.at[slot], out_h.at[slot], store_sem.at[1, slot]).wait()
 
+    @pl.when(is_even)
+    def _():
+        for slot in range(PATCHES):
+            for chunk in range(CHUNKS):
+                near_copy(slot, chunk).wait_send()
+                next_copy(slot, chunk, True).wait_send()
+
     @pl.when(sec < NSEC - 1)
     def _():
         for slot in range(PATCHES):
-            for tx in (tx_own, tx_near):
-                pltpu.make_async_remote_copy(
-                    src_ref=out_rows.at[slot], dst_ref=x_own.at[slot], send_sem=tx.at[slot], recv_sem=rx_own.at[slot],
-                    device_id=(up, blk), device_id_type=MESH,
-                ).wait_send()
+            for chunk in range(CHUNKS):
+                next_copy(slot, chunk, False).wait_send()
 
 
 def to_patch_order(order_s, rows_in, kv_in, rows_out, kv_out):
@@ -442,6 +506,7 @@
             pltpu.VMEM((2 * ROWS, D), bf16),
             pltpu.VMEM((ROWS, INNER), bf16),
             pltpu.VMEM((ROWS, INNER), bf16),
+            pltpu.VMEM((2 * (PATCHES - 1), ROWS, INNER), bf16),
             dma((NBLK,)),
             dma((NBLK,)),
             dma((NBLK,)),
@@ -454,13 +519,17 @@
             dma((62,)),
             dma((1,)),
             dma((4,)),
-            dma((PATCHES,)),
-            dma((PATCHES,)),
-            dma((PATCHES,)),
-            dma((PATCHES,)),
+            dma((PATCHES, CHUNKS)),
+            dma((PATCHES, CHUNKS)),
+            dma((PATCHES, CHUNKS)),
+            dma((PATCHES, CHUNKS)),
+            dma((PATCHES, CHUNKS)),
+            pltpu.SemaphoreType.REGULAR,
             dma((2, PATCHES)),
-            dma((2, PATCHES)),
-            dma((2, PATCHES)),
+            dma((2 * (PATCHES - 1),)),
+            dma((2 * (PATCHES - 1),)),
+            dma((2 * (PATCHES - 1),)),
+            dma((2 * (PATCHES - 1),)),
             dma(()),
             dma(()),
         ],

time: 332 us -> 320 us (0.964)
  the two profiles are of different devices: /device:TPU:103 before, /device:TPU:47 now
where the time goes in v3:
time: 320 us; the launch traced here: 319 us
  Pallas kernels  317 us (99%)
    pallas_call x1, Pallas kernels, on_device(): pl.pallas_call(kernel, out_shape=(jax.ShapeDtypeStruct((PATCHES, ROWS, D)...  311 us

profile of v3, /device:TPU:47, one launch (start us, length us, event | category | flops | bytes accessed | tf_op | source)
XLA Modules:
  0.0 319.5 jit_solution(10389844998701613224)
XLA Ops:
  0.6 1.2 copy.13
  1.8 0.9 reshape.21.mod_table
  2.7 311.1 %pipeline.1 = (bf16[4,128,1536]{2,1,0:T(8,128)(2,1)}, bf16[4,128,3072]{2,1,0:T(8,128)(2,1)}) custom-call(s32[4]{0:T(128)} %order_s.3, s32[4]{0:T(128)} %step_s.1, s32[4,8]{1,0:T(4,128)} %pattern_s.1, bf16[4,128,1536]{2,1,0:T(8,128)(2,1)} %bitcast.7, bf16[4,128,3072]{2,1,0:T(8,128)(2,1)} %bitcast.6, bf16[48,4608]{1,0:T(8,128)(2,1)} %bitcast.8, ...), custom_call_target="tpu_custom_call" | custom-call | tf_op jit(solution)/shard_map/pipeline/pallas_call | solution.py:484
  313.8 5.7 %patch_order.1 = (bf16[4,128,1536]{2,1,0:T(8,128)(2,1)}, bf16[4,128,3072]{2,1,0:T(8,128)(2,1)}) custom-call(s32[4]{0:T(128)} %order_s.3, bf16[4,128,1536]{2,1,0:T(8,128)(2,1)} %get-tuple-element.6.rows_in, bf16[4,128,3072]{2,1,0:T(8,128)(2,1)} %get-tuple-element.7.kv_in), custom_call_target="tpu_custom_call" | custom-call | tf_op jit(solution)/shard_map/patch_order/pallas_call | solution.py:552

commit v4 on v3

--- a/solution.py
+++ b/solution.py
@@ -1,3 +1,4 @@
+import functools
 import math
 
 import jax
@@ -24,10 +25,11 @@
 NORM_EPS = 1e-06
 CHUNK = 768
 CHUNKS = INNER // CHUNK
-SPLIT_QKV, SPLIT_OUT = 2560, 1024
+SPLIT = 2560
 OFFSETS = (0, 1, -1, 2, -2, 3, 4, 5)
 FAR_UP, FAR_DOWN = 5, 2
 PARTWAY = 2
+LAG = 1
 HELPED = 2
 HELPERS = NSEC - HELPED
 SCORE_SCALE = math.log2(math.e) / math.sqrt(HDIM)
@@ -49,7 +51,7 @@
     order_s, step_s, pattern_s, hidden_h, stale_h, wq_h, wo_h, qgain, kgain, mod_table,
     out_h, kv_h,
     wq, wo, wo_help, keys, values, x_own, x_near, mod_own, mod_near, stale, hidden, fresh, out_rows, modulated, queries, attended, relay,
-    recv_a, recv_b, recv_o, recv_p, recv_h, send_a, send_b, send_o, send_p, send_h, send_x, local, rx_own, rx_near, tx_own, tx_near, tx_next, go, store_sem, rx_stale, tx_stale, rx_relay, tx_relay, rx_mod, tx_mod,
+    recv_a, recv_b, recv_o, recv_h, send_a, send_b, send_o, send_h, send_x, local, rx_own, rx_near, tx_own, tx_near, tx_next, go, store_sem, rx_stale, tx_stale, rx_relay, tx_relay, rx_mod, tx_mod,
 ):
     sec = lax.axis_index("section")
     blk = lax.axis_index("blk")
@@ -129,6 +131,14 @@
                 self.push(there, ym)
             return here, there
 
+        def ring_step(self, k):
+            shard = at(y, z + OFFSETS[k])
+            self.arrived(shard)
+            self.along(shard, k)
+            self.push(shard, yp, ym)
+            if k > 0:
+                self.cross(k - 1, True)
+
         def wait_sends(self):
             for index in range(self.count):
                 pltpu.make_async_remote_copy(
@@ -136,38 +146,9 @@
                     recv_sem=self.recv.at[blk], device_id=(up, blk), device_id_type=MESH,
                 ).wait_send()
 
-    def gather(main, side, level, between=lambda k: None):
-        side.arrived(ym)
-        side.arrived(yp)
-        if level:
-            even = lax.rem(z, 2) == 0
-            side.push(jnp.where(even, ym, yp), jnp.where(even, yp, ym))
-        else:
-            side.push(yp, ym)
-        side.push(ym, zp, zm)
-        side.push(yp, zp, zm)
-        for k in range(1, NZ):
-            shard = at(y, z + OFFSETS[k])
-            main.arrived(shard)
-            main.along(shard, k)
-            main.push(shard, yp, ym)
-            if k == 1:
-                side.arrived(at(y + 2, z))
-                side.push(at(y + 2, z), zp, zm)
-            main.cross(k - 1, level)
-            for i in range(NY):
-                shard = at(y + i, z + OFFSETS[k])
-                side.arrived(shard)
-                side.along(shard, k)
-            between(k)
-        main.cross(NZ - 1, level)
-        for k in range(NZ):
-            main.arrived(at(y + 2, z + OFFSETS[k]))
-
-    qkv_main = Gather(wq, 0, SPLIT_QKV, recv_a, send_a, wq_h)
-    qkv_side = Gather(wq, SPLIT_QKV, 3 * INNER, recv_b, send_b, wq_h)
-    out_main = Gather(wo, 0, SPLIT_OUT, recv_o, send_o, wo_h)
-    out_side = Gather(wo, SPLIT_OUT, D, recv_p, send_p, wo_h)
+    main = Gather(wq, 0, SPLIT, recv_a, send_a, wq_h)
+    side = Gather(wq, SPLIT, 3 * INNER, recv_b, send_b, wq_h)
+    out = Gather(wo, 0, D, recv_o, send_o, wo_h)
     help_out = Gather(wo_help, 0, D, recv_h, send_h, wo_h)
     helped_out = Gather(wo, 0, D, recv_o, send_x, wo_h)
 
@@ -207,9 +188,13 @@
             help_out.push(shard, (chip_up, blk), to=helped_out)
 
     pl.when(sec == HELPERS)(let_go)
-    qkv_side.push(blk, yp, ym, from_input=True)
-    qkv_main.push(blk, zp, zm, yp, ym, from_input=True)
-    qkv_side.push(blk, zp, zm, from_input=True)
+    side.push(blk, yp, ym, from_input=True)
+    main.push(blk, zp, zm, yp, ym, from_input=True)
+    side.push(blk, zp, zm, from_input=True)
+
+    @pl.when(sec >= HELPED)
+    def _():
+        out.push(blk, zp, zm, yp, ym, from_input=True)
 
     for slot in range(PATCHES):
         step = step_s[order_s[slot]]
@@ -297,21 +282,44 @@
         if k == PARTWAY:
             pl.when(jnp.logical_and(is_even, sec < HELPERS))(let_go)
 
-    gather(qkv_main, qkv_side, False, between)
+    side.arrived(ym)
+    side.arrived(yp)
+    side.push(yp, ym)
+    side.push(ym, zp, zm)
+    side.push(yp, zp, zm)
+    for k in range(1, NZ):
+        shard = at(y, z + OFFSETS[k])
+        main.arrived(shard)
+        main.along(shard, k)
+        main.push(shard, yp, ym)
+        if k == 1:
+            side.arrived(at(y + 2, z))
+            side.push(at(y + 2, z), zp, zm)
+        main.cross(k - 1, False)
+        for i in range(NY):
+            shard = at(y + i, z + OFFSETS[k])
+            side.arrived(shard)
+            side.along(shard, k)
+        between(k)
+        if k > LAG:
+            pl.when(sec >= HELPED)(functools.partial(out.ring_step, k - LAG))
+    main.cross(NZ - 1, False)
+    for k in range(NZ):
+        main.arrived(at(y + 2, z + OFFSETS[k]))
     between(NZ)
 
     @pl.when(sec == 0)
     def _():
-        for slot in range(1, PATCHES):
-            for chunk in range(CHUNKS):
-                near_copy(slot, chunk).start()
+        for chunk in range(CHUNKS):
+            near_copy(1, chunk).start()
 
     @pl.when(sec >= HELPED)
     def _():
-        out_side.push(blk, yp, ym, from_input=True)
-        out_main.push(blk, zp, zm, yp, ym, from_input=True)
-        out_side.push(blk, zp, zm, from_input=True)
-        gather(out_main, out_side, True)
+        for k in range(NZ - LAG, NZ):
+            out.ring_step(k)
+        out.cross(NZ - 1, True)
+        for k in range(NZ):
+            out.arrived(at(y + 2, z + OFFSETS[k]))
 
     load_wq.wait()
     load_wo.wait()
@@ -325,12 +333,17 @@
             relay_copy(i, True).wait_send()
 
     def slot_step(slot, carry):
+        @pl.when(jnp.logical_and(sec == 0, slot < PATCHES - 2))
+        def _():
+            for chunk in range(CHUNKS):
+                near_copy(slot + 2, chunk).start()
+
         @pl.when(sec > 0)
         def _():
             for chunk in range(CHUNKS):
                 next_copy(slot, chunk, False).wait_recv()
 
-                @pl.when(is_even)
+                @pl.when(jnp.logical_and(is_even, slot == PATCHES - 1))
                 def _():
                     near_copy(slot, chunk).start()
 
@@ -434,19 +447,20 @@
 
         lax.fori_loop(0, CHUNKS, project_out, 0)
 
+        @pl.when(jnp.logical_and(jnp.logical_not(is_even), jnp.logical_and(sec < NSEC - 1, slot < PATCHES - 1)))
+        def _():
+            for chunk in range(CHUNKS):
+                next_copy(slot, chunk, True).start()
+
         pltpu.make_async_copy(out_rows.at[slot], out_h.at[slot], store_sem.at[1, slot]).start()
         return carry
 
     lax.fori_loop(0, PATCHES, slot_step, 0)
 
-    qkv_main.wait_sends()
-    qkv_side.wait_sends()
-
-    @pl.when(sec >= HELPED)
-    def _():
-        out_main.wait_sends()
-        out_side.wait_sends()
-
+    main.wait_sends()
+    side.wait_sends()
+
+    pl.when(sec >= HELPED)(out.wait_sends)
     pl.when(sec >= HELPERS)(help_out.wait_sends)
     pl.when(sec < HELPED)(helped_out.wait_sends)
 
@@ -454,11 +468,15 @@
         pltpu.make_async_copy(fresh.at[slot], kv_h.at[slot], store_sem.at[0, slot]).wait()
         pltpu.make_async_copy(out_rows.at[slot], out_h.at[slot], store_sem.at[1, slot]).wait()
 
-    @pl.when(is_even)
-    def _():
-        for slot in range(PATCHES):
+    for slot in range(PATCHES):
+        @pl.when(sec == 0 if slot < PATCHES - 1 else is_even)
+        def _():
             for chunk in range(CHUNKS):
                 near_copy(slot, chunk).wait_send()
+
+        @pl.when(sec < NSEC - 1 if slot < PATCHES - 1 else is_even)
+        def _():
+            for chunk in range(CHUNKS):
                 next_copy(slot, chunk, True).wait_send()
 
     @pl.when(sec < NSEC - 1)
@@ -511,8 +529,6 @@
             dma((NBLK,)),
             dma((NBLK,)),
             dma((NBLK,)),
-            dma((NBLK,)),
-            dma((31,)),
             dma((31,)),
             dma((31,)),
             dma((31,)),

time: 320 us -> 304 us (0.950)
  the two profiles are of different devices: /device:TPU:47 before, /device:TPU:103 now
where the time goes in v4:
time: 304 us; the launch traced here: 301 us
  Pallas kernels  298 us (98%)
    pallas_call x1, Pallas kernels, on_device(): pl.pallas_call(kernel, out_shape=(jax.ShapeDtypeStruct((PATCHES, ROWS, D)...  293 us

profile of v4, /device:TPU:103, one launch (start us, length us, event | category | flops | bytes accessed | tf_op | source)
XLA Modules:
  0.0 301.1 jit_solution(12178819201392289073)
XLA Ops:
  0.6 1.2 copy.13
  1.8 0.9 reshape.21.mod_table
  2.7 292.7 %pipeline.1 = (bf16[4,128,1536]{2,1,0:T(8,128)(2,1)}, bf16[4,128,3072]{2,1,0:T(8,128)(2,1)}) custom-call(s32[4]{0:T(128)} %order_s.3, s32[4]{0:T(128)} %step_s.1, s32[4,8]{1,0:T(4,128)} %pattern_s.1, bf16[4,128,1536]{2,1,0:T(8,128)(2,1)} %bitcast.7, bf16[4,128,3072]{2,1,0:T(8,128)(2,1)} %bitcast.6, bf16[48,4608]{1,0:T(8,128)(2,1)} %bitcast.8, ...), custom_call_target="tpu_custom_call" | custom-call | tf_op jit(solution)/shard_map/pipeline/pallas_call | solution.py:502
  295.4 5.7 %patch_order.1 = (bf16[4,128,1536]{2,1,0:T(8,128)(2,1)}, bf16[4,128,3072]{2,1,0:T(8,128)(2,1)}) custom-call(s32[4]{0:T(128)} %order_s.3, bf16[4,128,1536]{2,1,0:T(8,128)(2,1)} %get-tuple-element.6.rows_in, bf16[4,128,3072]{2,1,0:T(8,128)(2,1)} %get-tuple-element.7.kv_in), custom_call_target="tpu_custom_call" | custom-call | tf_op jit(solution)/shard_map/patch_order/pallas_call | solution.py:568

commit v5 on v4

--- a/solution.py
+++ b/solution.py
@@ -421,7 +421,7 @@
             attended[:, columns] = (mixture / weight_sum).astype(jnp.bfloat16)
             return carry
 
-        lax.fori_loop(0, HEADS, attend, 0, unroll=4)
+        lax.fori_loop(0, HEADS, attend, 0, unroll=6)
 
         def project_out(chunk, carry):
             columns = pl.ds(pl.multiple_of(chunk * CHUNK, CHUNK), CHUNK)

time: 304 us -> 307 us (level)
  no operation moved by 1% of the time
where the time goes in v5:
time: 307 us; the launch traced here: 304 us
  Pallas kernels  301 us (98%)
    pallas_call x1, Pallas kernels, on_device(): pl.pallas_call(kernel, out_shape=(jax.ShapeDtypeStruct((PATCHES, ROWS, D)...  296 us

profile of v5, /device:TPU:103, one launch (start us, length us, event | category | flops | bytes accessed | tf_op | source)
XLA Modules:
  0.0 303.9 jit_solution(13046057884502047833)
XLA Ops:
  0.6 1.2 copy.13
  1.8 0.9 reshape.21.mod_table
  2.7 295.6 %pipeline.1 = (bf16[4,128,1536]{2,1,0:T(8,128)(2,1)}, bf16[4,128,3072]{2,1,0:T(8,128)(2,1)}) custom-call(s32[4]{0:T(128)} %order_s.3, s32[4]{0:T(128)} %step_s.1, s32[4,8]{1,0:T(4,128)} %pattern_s.1, bf16[4,128,1536]{2,1,0:T(8,128)(2,1)} %bitcast.7, bf16[4,128,3072]{2,1,0:T(8,128)(2,1)} %bitcast.6, bf16[48,4608]{1,0:T(8,128)(2,1)} %bitcast.8, ...), custom_call_target="tpu_custom_call" | custom-call | tf_op jit(solution)/shard_map/pipeline/pallas_call | solution.py:502
  298.2 5.7 %patch_order.1 = (bf16[4,128,1536]{2,1,0:T(8,128)(2,1)}, bf16[4,128,3072]{2,1,0:T(8,128)(2,1)}) custom-call(s32[4]{0:T(128)} %order_s.3, bf16[4,128,1536]{2,1,0:T(8,128)(2,1)} %get-tuple-element.6.rows_in, bf16[4,128,3072]{2,1,0:T(8,128)(2,1)} %get-tuple-element.7.kv_in), custom_call_target="tpu_custom_call" | custom-call | tf_op jit(solution)/shard_map/patch_order/pallas_call | solution.py:568
